TPU v7x, 32 devices: a whole 2x2x4 slice. The times are simulated.
32 devices in a mesh: dp: 8 (over z, x), tensor: 4 (over y, core).
Axes of the slice: x: 2, y: 2, z: 4, core: 2. Of those that a mesh axis runs over, the one named last changes fastest.
Arguments:
- hidden_in: bfloat16 [1024, 32, 768], P('tensor', 'dp'), may hold values from -6 to 6
- cotangent: bfloat16 [1024, 32, 768], P('tensor', 'dp'), may hold values from -6 to 6
- prefix: int32 [32], P('dp'), may hold values from 102 to 512, as said below
- w_qkv: bfloat16 [768, 3, 768], P('dp', None, 'tensor'), may hold values from -0.21875 to 0.21875
- w_out: bfloat16 [768, 768], P('tensor', 'dp'), may hold values from -3 to 3
- w_in: bfloat16 [768, 3072], P('dp', 'tensor'), may hold values from -0.21875 to 0.21875
- w_down: bfloat16 [3072, 768], P('tensor', 'dp'), may hold values from -0.109375 to 0.109375
- biases: float32 [10, 768], P(None, ('dp', 'tensor')), may hold values from -1 to 1
- gains: float32 [2, 768], P(None, ('dp', 'tensor')), may hold values from 0.25 to 1.75
Outputs:
- output: bfloat16 [1024, 32, 768], P('tensor', 'dp')
- grad_input: bfloat16 [1024, 32, 768], P('tensor', 'dp')
- grad_qkv: float32 [768, 3, 768], P('dp', None, 'tensor')
- grad_out: float32 [768, 768], P('tensor', 'dp')
- grad_in: float32 [768, 3072], P('dp', 'tensor')
- grad_down: float32 [3072, 768], P('tensor', 'dp')
- grad_biases: float32 [10, 768], P(None, ('dp', 'tensor'))
- grad_gains: float32 [2, 768], P(None, ('dp', 'tensor'))
Inputs may be any that keep to these rules, and one draw needn't show every extreme that they name: Every draw has a sequence whose prefix is 512.
All inputs are finite; a program needn't handle non-finite values.
Results may differ from a plain program's by a relative error of at most 0.018.
Values may be sent and summed in bfloat16 or wider, within the bound.
A program may use at most 192 MiB of HBM per device.

v0:
```python
import functools
import math

import jax
import jax.numpy as jnp
from jax import lax
from jax.experimental import pallas as pl
from jax.experimental.pallas import tpu as pltpu
from jax.sharding import PartitionSpec as P

f32=jnp.float32; bf16=jnp.bfloat16
L=1024; QB=256; NK=(512,512,768,1024)
C2=0.125*math.log2(math.e)
NEG=-1e30
def dotf(a,b): return jnp.dot(a,b,preferred_element_type=f32)
def dot_nt(a,b): return lax.dot_general(a,b,(((1,),(1,)),((),())),preferred_element_type=f32)
def masks(mask_ref, prefix):
    k=lax.broadcasted_iota(jnp.int32,(256,256),0); q=lax.broadcasted_iota(jnp.int32,(256,256),1)
    diag=k<=q
    mask_ref[0]=jnp.where(diag|(k<prefix),0.0,NEG)
    mask_ref[1]=jnp.where(k+256<prefix,0.0,NEG)+jnp.zeros((256,256),f32)
    mask_ref[2]=jnp.where(diag|(k+256<prefix),0.0,NEG)
    mask_ref[3]=jnp.where(diag,0.0,NEG)
MASKMAP={0:{0:0,1:1},1:{1:2},2:{2:3},3:{3:3}}
def masked(st,qb,mask_ref):
    parts=[]
    for kb in range(NK[qb]//256):
        p=st[kb*256:(kb+1)*256]
        mi=MASKMAP[qb].get(kb)
        parts.append(p if mi is None else p+mask_ref[mi])
    return jnp.concatenate(parts,0)
def fwd_kernel(prefix_ref,x_ref,w_ref,b_ref,proj_ref,projT_ref,heads_ref,ot_ref,lse_ref,zq_ref,mask_ref):
    masks(mask_ref,prefix_ref[0])
    proj=(dotf(x_ref[...],w_ref[:,:640])+b_ref[...]).astype(bf16)
    proj_ref[...]=proj
    projT_ref[...]=proj.T
    zq_ref[...]=jnp.zeros_like(zq_ref)
    for h in range(3):
        zq_ref[h,64+64*h:128+64*h,:]=projT_ref[64*h:64*h+64,:]
    ot_ref[...]=jnp.zeros_like(ot_ref)
    for h in range(3):
        for qb in range(4):
            nk=NK[qb]; qs=slice(qb*QB,qb*QB+QB)
            st=dotf(proj_ref[:nk,128:384],zq_ref[h,:,qs])
            st=masked(st,qb,mask_ref)
            m=jnp.max(st,axis=0,keepdims=True)
            p=jnp.exp2((st-m)*C2)
            l=jnp.sum(p,axis=0,keepdims=True)
            ot=dotf(projT_ref[384+64*h:448+64*h,:nk],p.astype(bf16))
            ot_ref[64+64*h:128+64*h,qs]=(ot/l).astype(bf16)
            lse_ref[h:h+1,qs]=m*C2+jnp.log2(l)
    heads_ref[...]=ot_ref[...].T
def attn_fwd(prefix,x,w1,bqkv):
    sq=pl.squeezed
    return pl.pallas_call(fwd_kernel,grid_spec=pltpu.PrefetchScalarGridSpec(num_scalar_prefetch=1,grid=(4,),
      in_specs=[pl.BlockSpec((L,768),lambda t,p:(0,0)),pl.BlockSpec((sq,768,768),lambda t,p:(t,0,0)),pl.BlockSpec((sq,1,640),lambda t,p:(t,0,0))],
      out_specs=[pl.BlockSpec((sq,L,640),lambda t,p:(t,0,0)),pl.BlockSpec((sq,640,L),lambda t,p:(t,0,0)),pl.BlockSpec((sq,L,256),lambda t,p:(t,0,0)),pl.BlockSpec((sq,256,L),lambda t,p:(t,0,0)),pl.BlockSpec((sq,8,L),lambda t,p:(t,0,0))],
      scratch_shapes=[pltpu.VMEM((3,256,L),bf16),pltpu.VMEM((4,256,256),f32)]),
      out_shape=[jax.ShapeDtypeStruct((4,L,640),bf16),jax.ShapeDtypeStruct((4,640,L),bf16),jax.ShapeDtypeStruct((4,L,256),bf16),jax.ShapeDtypeStruct((4,256,L),bf16),jax.ShapeDtypeStruct((4,8,L),f32)],
      compiler_params=pltpu.CompilerParams(vmem_limit_bytes=62<<20))(prefix,x,w1,bqkv)
def bwd_kernel(prefix_ref,g_ref,w_ref,proj_ref,projT_ref,ot_ref,lse_ref,gproj_ref,
               zq_ref,zdo_ref,qm_ref,dom_ref,pt_ref,ds_ref,mask_ref,gt_ref,dqt_ref):
    masks(mask_ref,prefix_ref[0])
    gh=dotf(g_ref[...],w_ref[:,512:768]).astype(bf16)
    gt_ref[...]=gh.T
    zq_ref[...]=jnp.zeros_like(zq_ref); zdo_ref[...]=jnp.zeros_like(zdo_ref)
    lane=lax.broadcasted_iota(jnp.int32,(1,256),1)
    for h in range(3):
        zq_ref[h,64+64*h:128+64*h,:]=projT_ref[64*h:64*h+64,:]
        zdo_ref[h,64*h:64*h+64,:]=gt_ref[64+64*h:128+64*h,:]*0.125
        sel=(lane>=64*h)&(lane<64*h+64)
        qm_ref[h]=jnp.where(sel,proj_ref[:,0:256],0)
        sel2=(lane>=64*h+64)&(lane<64*h+128)
        dom_ref[h]=jnp.where(sel2,gh,0)
    for h in range(3):
        d=jnp.sum(gt_ref[64+64*h:128+64*h,:].astype(f32)*ot_ref[64+64*h:128+64*h,:].astype(f32),axis=0,keepdims=True)*0.125
        for qb in range(4):
            nk=NK[qb]; qs=slice(qb*QB,qb*QB+QB)
            st=dotf(proj_ref[:nk,128:384],zq_ref[h,:,qs])
            st=masked(st,qb,mask_ref)
            p=jnp.exp2(st*C2-lse_ref[h:h+1,qs])
            dp=dotf(proj_ref[:nk,384:640],zdo_ref[h,:,qs])
            ds=(p*(dp-d[:,qs])).astype(bf16)
            pt_ref[h,:nk,qs]=p.astype(bf16)
            ds_ref[h,:nk,qs]=ds
            dqt_ref[64*h:64*h+64,qs]=dotf(projT_ref[192+64*h:256+64*h,:nk],ds).astype(bf16)
    gproj_ref[:,0:192]=dqt_ref[...].T
    for (k0,k1,q0) in ((0,512,0),(512,768,512),(768,1024,768)):
        dk=jnp.zeros((k1-k0,256),f32); dv=jnp.zeros((k1-k0,256),f32)
        for h in range(3):
            dk=dk+dotf(ds_ref[h,k0:k1,q0:],qm_ref[h,q0:,:])
            dv=dv+dotf(pt_ref[h,k0:k1,q0:],dom_ref[h,q0:,:])
        gproj_ref[k0:k1,192:384]=dk[:,0:192].astype(bf16)
        gproj_ref[k0:k1,384:576]=dv[:,64:256].astype(bf16)
    gproj_ref[:,576:640]=jnp.zeros((L,64),bf16)
def attn_bwd(prefix,g,w1,proj,projT,ot,lse):
    sq=pl.squeezed
    sp=lambda *s: pl.BlockSpec((sq,)+s,lambda t,p:(t,0,0))
    return pl.pallas_call(functools.partial(bwd_kernel),grid_spec=pltpu.PrefetchScalarGridSpec(num_scalar_prefetch=1,grid=(4,),
      in_specs=[pl.BlockSpec((L,768),lambda t,p:(0,0)),sp(768,768),sp(L,640),sp(640,L),sp(256,L),sp(8,L)],
      out_specs=sp(L,640),
      scratch_shapes=[pltpu.VMEM((3,256,L),bf16),pltpu.VMEM((3,256,L),bf16),pltpu.VMEM((3,L,256),bf16),pltpu.VMEM((3,L,256),bf16),pltpu.VMEM((3,L,L),bf16),pltpu.VMEM((3,L,L),bf16),pltpu.VMEM((4,256,256),f32),pltpu.VMEM((256,L),bf16),pltpu.VMEM((192,L),bf16)]),
      out_shape=jax.ShapeDtypeStruct((4,L,640),bf16),
      compiler_params=pltpu.CompilerParams(vmem_limit_bytes=62<<20))(prefix,g,w1,proj,projT,ot,lse)
MESH=pl.DeviceIdType.MESH
class Place:
    def __init__(self):
        dp=lax.axis_index("dp"); t=lax.axis_index("tensor")
        self.dp,self.t=dp,t
        self.z,self.x,self.y,self.c=dp//2,dp%2,t//2,t%2
    def peer(self,dim,j=1):
        return {'x':lambda:(self.dp^1,self.t),'z':lambda:(self.dp^(2*j),self.t),'y':lambda:(self.dp,self.t^2),'c':lambda:(self.dp,self.t^1)}[dim]()
    def peers_all(self):
        return [self.peer('x'),self.peer('y'),self.peer('c'),self.peer('z',1),self.peer('z',2),self.peer('z',3),(self.dp,self.t^3)]
def barrier(peers):
    b=pltpu.get_barrier_semaphore()
    for p in peers: pl.semaphore_signal(b,inc=1,device_id=p,device_id_type=MESH)
    pl.semaphore_wait(b,len(peers))
class Sems:
    def __init__(self,send,recv): self.s,self.r,self.n=send,recv,0
    def take(self):
        i=self.n; self.n+=1
        return self.s.at[i],self.r.at[i]
def rcopy(src,dst,sems,dev):
    a,b=sems.take()
    return pltpu.make_async_remote_copy(src_ref=src,dst_ref=dst,send_sem=a,recv_sem=b,device_id=dev,device_id_type=MESH)
def local(src,dst,sem):
    k=pltpu.make_async_copy(src,dst,sem); k.start(); return k
def exchange(pc,src,dst,sems):
    out=[]
    for j in (2,3,1):
        p=(pc.dp,pc.t^j)
        k=rcopy(src.at[pc.t^j],dst.at[pc.t],sems,p); k.start(); out.append(k)
    return out
HBM=pl.BlockSpec(memory_space=pltpu.HBM); VM=pl.BlockSpec(memory_space=pltpu.VMEM)
def point(steps, k, h):
    for kk in range(4):
        todo = steps.get((kk, h))
        if todo:
            @pl.when(k == kk)
            def _(todo=todo):
                for step in todo:
                    step()


def add_into(dst, src, n, pick_dst, pick_src):
    def body(j, _):
        a, b = pick_dst(j), pick_src(j)
        dst[a] = (dst[a].astype(f32) + src[b].astype(f32)).astype(bf16)
        return 0
    lax.fori_loop(0, n, body, 0)


class Reduce:
    def __init__(self, pc, d_ref, half, lc, rc, r1, r2, r3, sems, lsem):
        self.pc, self.lc, self.rc, self.r1, self.r2, self.r3 = pc, lc, rc, r1, r2, r3
        rows = pl.ds(48 * half, 48)
        self.own = pltpu.make_async_copy(d_ref.at[:, pc.c, :, :, rows], lc, lsem)
        self.q0 = rcopy(d_ref.at[:, 1 - pc.c, :, :, rows], rc, sems, pc.peer("c"))
        self.q1 = rcopy(lc.at[:, :, 1 - pc.x], r1, sems, pc.peer("x"))
        self.q2 = [rcopy(lc.at[:, pc.z ^ j, pc.x], r2.at[j - 1], sems, pc.peer("z", j)) for j in (3, 2, 1)]
        self.q3 = rcopy(lc.at[1 - pc.y, pc.z, pc.x], r3, sems, pc.peer("y"))

    def s0(self):
        self.own.start()
        self.q0.start()

    def s1(self):
        self.own.wait()
        self.q0.wait_recv()
        at = lambda j: (j // 8, (j // 2) % 4, j % 2)
        add_into(self.lc, self.rc, 16, at, at)
        self.q1.start()

    def s2(self):
        self.q1.wait_recv()
        add_into(self.lc, self.r1, 8, lambda j: (j // 4, j % 4, self.pc.x), lambda j: (j // 4, j % 4))
        for q in self.q2:
            q.start()

    def s3(self):
        pc = self.pc
        for q in self.q2:
            q.wait_recv()
        for y in range(2):
            at = (y, pc.z, pc.x)
            total = (self.lc[at].astype(f32) + self.r2[0, y].astype(f32)) + (self.r2[1, y].astype(f32) + self.r2[2, y].astype(f32))
            self.lc[at] = total.astype(bf16)
        self.q3.start()

    def s4(self, out_ref, rows):
        pc = self.pc
        self.q3.wait_recv()
        out_ref[rows] = self.lc[pc.y, pc.z, pc.x].astype(f32) + self.r3[...].astype(f32)

    def end(self):
        for q in [self.q0, self.q1, self.q3] + self.q2:
            q.wait_send()


N_C = 4 * 6 + 1 + 1 + 1 + 2 + 6 + 6 + 6


def back_kernel(
    prefix_ref, x_ref, g_ref, gf_ref, w_ref, proj_ref, projT_ref, ot_ref, lse_ref, dout_ref, d_ref, v_ref, out_ref,
    gs_ref, vs_ref, oo_ref, xo_ref,
    xT, gl, dxa, w_b, proj_b, projT_b, ot_b, lse_b, dout_b,
    zq, zdo, qm, dom, pt, ds, mask_ref, gt, dqt, dkb, dvb, gproj,
    lc, rc, r1, r2, r3, dwb, cr, yr, xr, zr, vb, vr, xst, ss, rs, ls, ins,
):
    pc = Place()
    sems = Sems(ss, rs)
    w1 = w_ref.at[0]
    lane = lax.broadcasted_iota(jnp.int32, (1, 256), 1)

    def loads(k, slot):
        t = pc.t ^ (3 - k)
        pairs = [
            (w1.at[t // 2, t % 2], w_b), (proj_ref.at[t], proj_b), (projT_ref.at[t], projT_b),
            (ot_ref.at[t], ot_b), (lse_ref.at[t], lse_b), (dout_ref.at[t], dout_b),
        ]
        return [pltpu.make_async_copy(a, b.at[slot], ins.at[slot, n]) for n, (a, b) in enumerate(pairs)]

    first = loads(0, 0)
    for q in first:
        q.start()
    l_x = local(x_ref, xst, ls.at[4])
    l_g = local(g_ref, gl, ls.at[5])
    l_f = local(gf_ref, dxa, ls.at[6])
    barrier(pc.peers_all())
    red = {}
    for n, (g, i) in enumerate(((1, 0), (1, 1), (0, 0), (0, 1))):
        red[n] = Reduce(pc, d_ref.at[g], i, lc.at[n], rc.at[n], r1.at[n], r2.at[n], r3.at[n], sems, ls.at[n])
        red[n].s0()
    ox = exchange(pc, out_ref, oo_ref, sems)
    l_o = [local(out_ref.at[pc.t], oo_ref.at[pc.t], ls.at[7])]
    q_c0 = rcopy(dwb.at[0], cr.at[0], sems, pc.peer("c"))
    q_y = rcopy(dwb.at[1], yr, sems, pc.peer("y"))
    q_c1 = rcopy(dwb.at[2], cr.at[1], sems, pc.peer("c"))
    half = [pl.ds(48 * i, 48) for i in range(2)]
    q_x = [rcopy(dwb.at[3, :, 1 - pc.x, half[i]], xr.at[i], sems, pc.peer("x")) for i in range(2)]
    q_z = [[rcopy(dwb.at[3, pc.z ^ j, pc.x, half[i]], zr.at[i, j - 1], sems, pc.peer("z", j)) for j in (3, 2, 1)] for i in range(2)]
    steps = {
        (0, 1): [red[0].s1], (0, 2): [red[1].s1], (0, 3): [red[2].s1], (1, 1): [red[3].s1],
        (1, 3): [red[0].s2], (2, 3): [red[1].s2], (3, 0): [red[0].s3], (3, 3): [red[2].s2],
    }
    masks(mask_ref, prefix_ref[0])
    zq[...] = jnp.zeros_like(zq)
    zdo[...] = jnp.zeros_like(zdo)
    gproj[:, 576:640] = jnp.zeros((L, 64), bf16)
    vb[0] = v_ref[...]
    l_x.wait()
    xT[...] = xst[...].reshape(L, 768).T
    l_g.wait()
    l_f.wait()

    def group(k, _):
        slot = k % 2
        for q in loads(k, slot):
            q.wait()

        @pl.when(k < 3)
        def _():
            for q in loads(k + 1, 1 - slot):
                q.start()

        t = pc.t ^ (3 - k)
        w, pj, pjT, o_t, lse = w_b.at[slot], proj_b.at[slot], projT_b.at[slot], ot_b.at[slot], lse_b.at[slot]
        gh = dotf(gl[...], w[...].reshape(768, 768)[:, 512:768]).astype(bf16)
        gt[...] = gh.T
        for h in range(3):
            point(steps, k, h)
            own = slice(64 + 64 * h, 128 + 64 * h)
            zq[h, own, :] = pjT[64 * h : 64 * h + 64, :]
            zdo[h, 64 * h : 64 * h + 64, :] = gt[own, :] * 0.125
            qm[...] = jnp.where((lane >= 64 * h) & (lane < 64 * h + 64), pj[:, 0:256], 0)
            dom[...] = jnp.where((lane >= 64 * h + 64) & (lane < 64 * h + 128), gh, 0)
            d = jnp.sum(gt[own, :].astype(f32) * o_t[own, :].astype(f32), axis=0, keepdims=True) * 0.125
            for qb in range(4):
                nk = NK[qb]
                qs = slice(qb * QB, qb * QB + QB)
                st = masked(dotf(pj[:nk, 128:384], zq[h, :, qs]), qb, mask_ref)
                p = jnp.exp2(st * C2 - lse[h : h + 1, qs])
                dp = dotf(pj[:nk, 384:640], zdo[h, :, qs])
                dsv = (p * (dp - d[:, qs])).astype(bf16)
                pt[:nk, qs] = p.astype(bf16)
                ds[:nk, qs] = dsv
                dqt[64 * h : 64 * h + 64, qs] = dotf(pjT[192 + 64 * h : 256 + 64 * h, :nk], dsv).astype(bf16)
            for k0, k1, q0 in ((0, 512, 0), (512, 768, 512), (768, 1024, 768)):
                dk = dotf(ds[k0:k1, q0:], qm[q0:, :]).astype(bf16)
                dv = dotf(pt[k0:k1, q0:], dom[q0:, :]).astype(bf16)
                dkb[k0:k1] = dk if h == 0 else dkb[k0:k1] + dk
                dvb[k0:k1] = dv if h == 0 else dvb[k0:k1] + dv
        point(steps, k, 3)
        gproj[:, 0:192] = dqt[...].T
        gproj[:, 192:384] = dkb[:, 0:192]
        gproj[:, 384:576] = dvb[:, 64:256]
        vb[0, pl.ds(16 + 2 * t, 1), 0:256] = jnp.sum(gproj[:, 0:256].astype(f32), axis=0, keepdims=True)
        vb[0, pl.ds(17 + 2 * t, 1), 0:256] = jnp.sum(gproj[:, 384:640].astype(f32), axis=0, keepdims=True)
        dw = dotf(xT[...], gproj[...])
        do = dout_b[slot].astype(f32)
        shape = lambda a: a.astype(bf16).reshape(4, 2, 96, a.shape[1])
        dwb[k, :, :, :, 0:512] = shape(dw[:, 0:512])
        dwb[k, :, :, :, 512:640] = shape(dw[:, 512:640] + do[:, 0:128])
        dwb[k, :, :, :, 640:768] = shape(do[:, 128:256])

        @pl.when(k == 0)
        def _():
            q_c0.start()

        @pl.when(k == 1)
        def _():
            q_c0.wait_recv()
            add_into(dwb.at[1], cr.at[0], 8, lambda j: (j // 2, j % 2), lambda j: (j // 2, j % 2))
            q_y.start()

        @pl.when(k == 2)
        def _():
            q_c1.start()

        @pl.when(k == 3)
        def _():
            q_c1.wait_recv()
            add_into(dwb.at[3], cr.at[1], 8, lambda j: (j // 2, j % 2), lambda j: (j // 2, j % 2))
            q_y.wait_recv()
            add_into(dwb.at[3], yr, 8, lambda j: (j // 2, j % 2), lambda j: (j // 2, j % 2))
            for q in q_x:
                q.start()

        dxa[...] += dot_nt(gproj[...], w[...].reshape(768, 768)[:, 0:640])
        return 0

    lax.fori_loop(0, 4, group, 0)
    xst[...] = dxa[...].astype(bf16).reshape(4, 256, 768)
    v_q = [rcopy(vb.at[0], vr.at[0], sems, pc.peer("c"))]
    v_q[0].start()
    xx = exchange(pc, xst, xo_ref, sems)
    l_o.append(local(xst.at[pc.t], xo_ref.at[pc.t], ls.at[8]))

    def vstep(n, dim):
        v_q[n].wait_recv()
        vb[n + 1] = vb[n] + vr[n]
        v_q.append(rcopy(vb.at[n + 1], vr.at[n + 1], sems, pc.peer(dim)))
        v_q[n + 1].start()

    vstep(0, "x")
    red[1].s3()
    for i in range(2):
        q_x[i].wait_recv()
        for z in range(4):
            dwb[3, z, pc.x, half[i]] = (dwb[3, z, pc.x, half[i]].astype(f32) + xr[i, z].astype(f32)).astype(bf16)
        for q in q_z[i]:
            q.start()
    vstep(1, "y")
    red[3].s2()
    red[2].s3()
    v_q[2].wait_recv()
    vb[3] = vb[2] + vr[2]
    v_z = [rcopy(vb.at[3], vr.at[2 + j], sems, pc.peer("z", j)) for j in (3, 2, 1)]
    for q in v_z:
        q.start()
    red[0].s4(gs_ref.at[2], slice(0, 48))
    red[1].s4(gs_ref.at[2], slice(48, 96))
    red[3].s3()
    for i in range(2):
        for q in q_z[i]:
            q.wait_recv()
        gs_ref[0, 48 * i : 48 * i + 48] = (dwb[3, pc.z, pc.x, half[i]].astype(f32) + zr[i, 0].astype(f32)) + (zr[i, 1].astype(f32) + zr[i, 2].astype(f32))
    red[2].s4(gs_ref.at[1], slice(0, 48))
    for q in v_z:
        q.wait_recv()
    vs_ref[...] = (vb[3] + vr[3]) + (vr[4] + vr[5])
    red[3].s4(gs_ref.at[1], slice(48, 96))
    for q in l_o:
        q.wait()
    for q in ox + xx:
        q.wait()
    for n in range(4):
        red[n].end()
    for q in [q_c0, q_y, q_c1] + q_x + q_z[0] + q_z[1] + v_q + v_z:
        q.wait_send()


def back(prefix, x, g1low, g1, g, proj, projT, ot, lse, doutw, d, v, out4):
    v_ = pltpu.VMEM
    dma = pltpu.SemaphoreType.DMA
    sd = jax.ShapeDtypeStruct
    return pl.pallas_call(
        back_kernel,
        out_shape=[sd((3, 96, 768), f32), sd((24, 768), f32), sd((4, 256, 768), bf16), sd((4, 256, 768), bf16)],
        in_specs=[pl.BlockSpec(memory_space=pltpu.SMEM)] + [HBM] * 10 + [VM, HBM],
        out_specs=[VM, VM, HBM, HBM],
        scratch_shapes=[
            v_((768, L), bf16), v_((L, 768), bf16), v_((L, 768), f32),
            v_((2, 4, 2, 96, 768), bf16), v_((2, L, 640), bf16), v_((2, 640, L), bf16), v_((2, 256, L), bf16), v_((2, 8, L), f32), v_((2, 768, 256), bf16),
            v_((3, 256, L), bf16), v_((3, 256, L), bf16), v_((L, 256), bf16), v_((L, 256), bf16), v_((L, L), bf16), v_((L, L), bf16),
            v_((4, 256, 256), f32), v_((256, L), bf16), v_((192, L), bf16), v_((L, 256), bf16), v_((L, 256), bf16), v_((L, 640), bf16),
            v_((4, 2, 4, 2, 48, 768), bf16), v_((4, 2, 4, 2, 48, 768), bf16), v_((4, 2, 4, 48, 768), bf16), v_((4, 3, 2, 48, 768), bf16), v_((4, 48, 768), bf16),
            v_((4, 4, 2, 96, 768), bf16), v_((2, 4, 2, 96, 768), bf16), v_((4, 2, 96, 768), bf16), v_((2, 4, 48, 768), bf16), v_((2, 3, 48, 768), bf16),
            v_((4, 24, 768), f32), v_((6, 24, 768), f32), v_((4, 256, 768), bf16),
            dma((N_C,)), dma((N_C,)), dma((9,)), dma((2, 6)),
        ],
        compiler_params=pltpu.CompilerParams(collective_id=1, has_side_effects=True, vmem_limit_bytes=67043328),
    )(prefix, x, g1low, g1, g, proj, projT, ot, lse, doutw, d, v, out4)


class Gather:
    def __init__(self, pc, src, dst, rows, order, sems):
        self.pc, self.src, self.dst, self.rows, self.order, self.sems = pc, src, dst, rows, order, sems
        self.full, self.sent, self.core = set(), [], []
        self.plan()

    def at(self, over, full):
        pc = self.pc
        ix = {d: over.get(d, slice(None) if d in full else getattr(pc, d)) for d in "yzx"}
        return self.dst.at[(ix["y"], pc.c, ix["z"], ix["x"]) + ((pl.ds(*self.rows),) if self.rows else ())]

    def plan(self):
        pc = self.pc
        src = self.src.at[pl.ds(*self.rows)] if self.rows else self.src
        mine = self.at({}, set())
        self.core.append(rcopy(src, mine, self.sems, pc.peer("c")))
        self.phases = []
        full = set()
        for d in self.order:
            ks = []
            for j in (1, 2, 3) if d == "z" else (1,):
                here = self.at({}, full)
                ks.append(rcopy(here if full else src, here, self.sems, pc.peer(d, j)))
                there = self.at({d: getattr(pc, d) ^ j}, full)
                self.core.append(rcopy(there, there, self.sems, pc.peer("c")))
            self.phases.append(ks)
            full = full | {d}
        self.first = [1]
        for ks in self.phases:
            self.first.append(self.first[-1] + len(ks))

    def start(self):
        self.core[0].start()
        for k in self.phases[0]:
            k.start()

    def arrive(self, p):
        for n, k in enumerate(self.phases[p]):
            k.wait_recv()
            self.core[self.first[p] + n].start()

    def next(self, p):
        self.arrive(p - 1)
        for k in self.phases[p]:
            k.start()

    def from_core(self, a, b):
        for k in self.core[a:b]:
            k.wait_recv()

    def end(self):
        for k in self.core + sum(self.phases, []):
            k.wait_send()


N_A = 6 * 11 + 6


def front_kernel(
    prefix_ref, s_ref, h_ref, c_ref, b_ref,
    g_ref, x_ref, co_ref, vec_ref, proj_ref, projT_ref, heads_ref, ot_ref, lse_ref,
    bv, sv, xv, cst, wv, proj_b, projT_b, heads_b, ot_b, lse_b, zq, mask_ref, ss, rs, ls, os_,
):
    pc = Place()
    sems = Sems(ss, rs)
    own = (pc.y, pc.c, pc.z, pc.x)
    l_s = local(s_ref, sv, ls.at[0])
    l_h = local(h_ref.at[pc.t], xv.at[pc.t], ls.at[1])
    l_c = local(c_ref.at[pc.t], cst, ls.at[2])
    l_b = local(b_ref, bv.at[own], ls.at[9])
    barrier(pc.peers_all())
    bias = Gather(pc, b_ref, bv, None, "zxy", sems)
    w1 = Gather(pc, s_ref.at[0], g_ref.at[0], None, "zxy", sems)
    w2 = [Gather(pc, s_ref.at[1], g_ref.at[1], (48 * i, 48), "yzx", sems) for i in range(2)]
    w3 = [Gather(pc, s_ref.at[2], g_ref.at[2], (48 * i, 48), "yzx", sems) for i in range(2)]
    bias.start()
    w1.start()
    w2[0].start()
    w2[1].start()
    hx = exchange(pc, h_ref, xv, sems)
    w3[0].start()
    w3[1].start()
    l_s.wait()
    l_g = [local(sv.at[g], g_ref.at[g].at[own], ls.at[3 + g]) for g in range(3)]
    l_c.wait()
    l_c2 = local(cst, co_ref.at[pc.t], ls.at[6])
    masks(mask_ref, prefix_ref[0])
    zq[...] = jnp.zeros_like(zq)
    ot_b[...] = jnp.zeros_like(ot_b)
    for q in l_g:
        q.wait()
    l_b.wait()
    w1.next(1)
    bias.next(1)
    w2[0].next(1)
    w1.next(2)
    bias.next(2)
    w2[1].next(1)
    bias.arrive(2)
    bias.from_core(0, len(bias.core))
    l_h.wait()
    for q in hx:
        q.wait_recv()
    l_x = local(xv, x_ref, ls.at[7])
    c_plan = [rcopy(c_ref.at[pc.t ^ j], co_ref.at[pc.t], sems, (pc.dp, pc.t ^ j)) for j in (2, 3, 1)]

    def load(k, slot):
        t = pc.t ^ k
        return pltpu.make_async_copy(g_ref.at[0, t // 2, t % 2], wv.at[slot], ls.at[8])

    def start_cot():
        for q in c_plan:
            q.start()

    steps = {
        (0, 1): [lambda: w3[0].next(1), lambda: w3[1].next(1)],
        (0, 2): [lambda: w1.from_core(0, 5), lambda: load(1, 1).start()],
        (1, 0): [lambda: w2[0].next(2)],
        (1, 1): [start_cot],
        (1, 3): [lambda: w1.arrive(2), lambda: load(2, 0).start()],
        (2, 0): [lambda: w2[1].next(2)],
        (2, 2): [lambda: w1.from_core(5, 6), lambda: load(3, 1).start()],
        (3, 2): [lambda: w3[0].next(2)],
    }
    load(0, 0).start()

    def outs(k, slot):
        t = pc.t ^ k
        pairs = [(proj_b, proj_ref), (projT_b, projT_ref), (heads_b, heads_ref), (ot_b, ot_ref), (lse_b, lse_ref)]
        return [pltpu.make_async_copy(a.at[slot], b.at[t], os_.at[slot, n]) for n, (a, b) in enumerate(pairs)]

    def group(k, _):
        slot = k % 2
        t = pc.t ^ k
        load(k, slot).wait()

        @pl.when(k >= 2)
        def _():
            for q in outs(k - 2, slot):
                q.wait()

        row = jnp.zeros((8, 256), f32)
        for i in range(8):
            piece = bv[(i // 2) % 2, i % 2, t, i // 4, 0:8, :]
            row = row + pltpu.roll(jnp.concatenate([piece, jnp.zeros((8, 128), f32)], 1), 24 * i, 1)
        brow = jnp.concatenate([row[0:1], jnp.zeros((1, 128), f32), row[1:2]], 1)
        pj, pjT, ot, lse = proj_b.at[slot], projT_b.at[slot], ot_b.at[slot], lse_b.at[slot]
        proj = (dotf(xv[...].reshape(L, 768), wv[slot].reshape(768, 768)[:, :640]) + brow).astype(bf16)
        pj[...] = proj
        pjT[...] = proj.T
        for h in range(3):
            point(steps, k, h)
            zq[h, 64 + 64 * h : 128 + 64 * h, :] = pjT[64 * h : 64 * h + 64, :]
            for qb in range(4):
                nk = NK[qb]
                qs = slice(qb * QB, qb * QB + QB)
                st = masked(dotf(pj[:nk, 128:384], zq[h, :, qs]), qb, mask_ref)
                m = jnp.max(st, axis=0, keepdims=True)
                p = jnp.exp2((st - m) * C2)
                l = jnp.sum(p, axis=0, keepdims=True)
                o = dotf(pjT[384 + 64 * h : 448 + 64 * h, :nk], p.astype(bf16))
                ot[64 + 64 * h : 128 + 64 * h, qs] = (o / l).astype(bf16)
                lse[h : h + 1, qs] = m * C2 + jnp.log2(l)
        point(steps, k, 3)
        heads_b[slot] = ot[...].T
        for q in outs(k, slot):
            q.start()
        return 0

    lax.fori_loop(0, 4, group, 0)
    w3[1].next(2)
    tiles = [jnp.zeros((16, 128), f32) for _ in range(6)]
    lane = lax.broadcasted_iota(jnp.int32, (1, 128), 1)
    for i in range(32):
        z, x, y, c = i // 8, (i // 4) % 2, (i // 2) % 2, i % 2
        j, r = (24 * i) // 128, (24 * i) % 128
        piece = pltpu.roll(bv[y, c, z, x], r, 1) if r else bv[y, c, z, x]
        tiles[j] = tiles[j] + (jnp.where(lane >= r, piece, 0.0) if r > 104 else piece)
        if r > 104:
            tiles[j + 1] = tiles[j + 1] + jnp.where(lane < r, piece, 0.0)
    for j in range(6):
        vec_ref[:, 128 * j : 128 * j + 128] = tiles[j]
    for g in w2 + w3:
        g.arrive(2)
    for g in w2 + w3:
        g.from_core(0, 6)
    for q in hx:
        q.wait_send()
    for q in c_plan:
        q.wait()
    l_x.wait()
    l_c2.wait()
    for k in (2, 3):
        for q in outs(k, k % 2):
            q.wait()
    for g in [bias, w1] + w2 + w3:
        g.end()


def front(prefix, s, h, c, b):
    v_ = pltpu.VMEM
    dma = pltpu.SemaphoreType.DMA
    sd = jax.ShapeDtypeStruct
    return pl.pallas_call(
        front_kernel,
        out_shape=[
            sd((3, 2, 2, 4, 2, 96, 768), bf16), sd((4, 256, 768), bf16), sd((4, 256, 768), bf16), sd((16, 768), f32),
            sd((4, L, 640), bf16), sd((4, 640, L), bf16), sd((4, L, 256), bf16), sd((4, 256, L), bf16), sd((4, 8, L), f32),
        ],
        in_specs=[pl.BlockSpec(memory_space=pltpu.SMEM)] + [HBM] * 3 + [VM],
        out_specs=[HBM] * 3 + [VM] + [HBM] * 5,
        scratch_shapes=[
            v_((2, 2, 4, 2, 16, 128), f32), v_((3, 96, 768), bf16), v_((4, 256, 768), bf16), v_((256, 768), bf16), v_((2, 4, 2, 96, 768), bf16),
            v_((2, L, 640), bf16), v_((2, 640, L), bf16), v_((2, L, 256), bf16), v_((2, 256, L), bf16), v_((2, 8, L), f32),
            v_((3, 256, L), bf16), v_((4, 256, 256), f32),
            dma((N_A,)), dma((N_A,)), dma((10,)), dma((2, 5)),
        ],
        compiler_params=pltpu.CompilerParams(collective_id=0, has_side_effects=True, vmem_limit_bytes=67043328),
    )(prefix, s, h, c, b)


EPSILON = 1e-12


def gelu_pair(v):
    cdf = 0.5 + 0.5 * lax.erf(v * math.sqrt(0.5))
    pdf = jnp.exp2(v * v * (-0.5 * math.log2(math.e))) * (1.0 / math.sqrt(2.0 * math.pi))
    return v * cdf, cdf + v * pdf


def row_mean(a):
    return jnp.sum(a, axis=-1, keepdims=True) * (1.0 / 768.0)


def mid_kernel(
    x_ref, c_ref, heads_ref, g_ref, vec_ref,
    out_ref, g1_ref, g1low_ref, dout_ref, d_ref, v_ref,
    xv, cv, hv, wo, w2, w3, xhat, inv, low, act, gd, acc, glow, lowT, gT, stage, dst, ls, ds_,
):
    l_x = local(x_ref, xv, ls.at[0])
    l_h = local(heads_ref, hv, ls.at[1])
    l_wo = [local(g_ref.at[0, y, c, :, :, :, pl.ds(512, 256)], wo.at[2 * y + c], ls.at[2 + 2 * y + c]) for y in range(2) for c in range(2)]
    l_w2 = local(g_ref.at[1], w2, ls.at[6])
    l_w3 = local(g_ref.at[2], w3, ls.at[7])
    l_c = local(c_ref, cv, ls.at[8])
    row = lambda n: vec_ref[n : n + 1, :]
    v_ref[...] = jnp.zeros_like(v_ref)

    def add_row(n, a):
        v_ref[n : n + 1, :] += jnp.sum(a, axis=0, keepdims=True)

    for q in [l_x, l_h] + l_wo:
        q.wait()

    def first(b, _):
        rows = pl.ds(pl.multiple_of(b * 256, 256), 256)
        r = xv[b].astype(f32) + row(2)
        for t in range(4):
            r = r + dot_nt(hv[t, rows, :], wo[t].reshape(768, 256))
        center = r - row_mean(r)
        iv = lax.rsqrt(row_mean(center * center) + EPSILON)
        xh = center * iv
        xhat[rows, :] = xh
        inv[rows, :] = jnp.broadcast_to(iv, (256, 128))
        normed = xh * row(10) + row(8)
        low[rows, :] = normed.astype(bf16)
        acc[rows, :] = normed + row(7)
        return 0

    lax.fori_loop(0, 4, first, 0)
    l_w2.wait()
    l_w3.wait()

    def up(n, _):
        t, b = n // 4, n % 4
        rows = pl.ds(pl.multiple_of(b * 256, 256), 256)
        pre = dotf(low[rows, :], w2[t // 2, t % 2].reshape(768, 768)) + vec_ref[pl.ds(3 + t, 1), :]
        a, d = gelu_pair(pre)
        a = a.astype(bf16)
        act[t, rows, :] = a
        gd[t, rows, :] = d.astype(bf16)
        acc[rows, :] += dot_nt(a, w3[t // 2, t % 2].reshape(768, 768))
        return 0

    lax.fori_loop(0, 16, up, 0)
    l_c.wait()

    def second(b, _):
        rows = pl.ds(pl.multiple_of(b * 256, 256), 256)
        r = acc[rows, :]
        center = r - row_mean(r)
        iv = lax.rsqrt(row_mean(center * center) + EPSILON)
        xh = center * iv
        stage[b] = (xh * row(11) + row(9)).astype(bf16)
        ct = cv[b].astype(f32)
        e = ct * row(11)
        g2 = (e - row_mean(e) - xh * row_mean(e * xh)) * iv
        acc[rows, :] = g2
        glow[rows, :] = g2.astype(bf16)
        add_row(11, ct * xh)
        add_row(9, ct)
        add_row(7, g2)
        return 0

    lax.fori_loop(0, 4, second, 0)
    l_o = local(stage, out_ref, ls.at[0])
    gT[...] = glow[...].T
    lowT[...] = low[...].T

    def sends(t):
        return [pltpu.make_async_copy(dst.at[t % 2, n], d_ref.at[n, t], ds_.at[t % 2, n]) for n in range(2)]

    def down(t, _):
        wt2, wt3 = w2.at[t // 2, t % 2], w3.at[t // 2, t % 2]

        @pl.when(t >= 2)
        def _():
            for q in sends(t - 2):
                q.wait()

        dst[t % 2, 1] = dotf(gT[...], act[t]).astype(bf16)
        for b in range(4):
            rows = slice(256 * b, 256 * b + 256)
            ga = dotf(glow[rows, :], wt3[...].reshape(768, 768))
            gp = (ga * gd[t, rows, :].astype(f32)).astype(bf16)
            gd[t, rows, :] = gp
            acc[rows, :] += dot_nt(gp, wt2[...].reshape(768, 768))
            v_ref[pl.ds(3 + t, 1), :] += jnp.sum(gp.astype(f32), axis=0, keepdims=True)
        dst[t % 2, 0] = dotf(lowT[...], gd[t]).astype(bf16)
        for q in sends(t):
            q.start()
        return 0

    lax.fori_loop(0, 4, down, 0)

    def last(b, _):
        rows = pl.ds(pl.multiple_of(b * 256, 256), 256)
        gn, xh = acc[rows, :], xhat[rows, :]
        e = gn * row(10)
        g1 = (e - row_mean(e) - xh * row_mean(e * xh)) * inv[rows, 0:1]
        acc[rows, :] = g1
        glow[rows, :] = g1.astype(bf16)
        add_row(10, gn * xh)
        add_row(8, gn)
        add_row(2, g1)
        return 0

    lax.fori_loop(0, 4, last, 0)
    l_g = [local(acc, g1_ref, ls.at[1]), local(glow, g1low_ref, ls.at[2])]
    gT[...] = glow[...].T
    for q in sends(2) + sends(3):
        q.wait()
    for t in range(4):
        dst[t // 2, t % 2, :, 0:256] = dotf(gT[...], hv[t]).astype(bf16)
    l_d = [local(dst.at[t // 2, t % 2, :, pl.ds(0, 256)], dout_ref.at[t], ls.at[3 + t]) for t in range(4)]
    for q in [l_o] + l_g + l_d:
        q.wait()


def mid(xs, cs, heads, g, vec):
    v_ = pltpu.VMEM
    dma = pltpu.SemaphoreType.DMA
    sd = jax.ShapeDtypeStruct
    wt = v_((2, 2, 4, 2, 96, 768), bf16)
    return pl.pallas_call(
        mid_kernel,
        out_shape=[sd((4, 256, 768), bf16), sd((L, 768), f32), sd((L, 768), bf16), sd((4, 768, 256), bf16), sd((2, 4, 768, 768), bf16), sd((24, 768), f32)],
        in_specs=[HBM] * 4 + [VM],
        out_specs=[HBM] * 5 + [VM],
        scratch_shapes=[
            v_((4, 256, 768), bf16), v_((4, 256, 768), bf16), v_((4, L, 256), bf16), v_((4, 4, 2, 96, 256), bf16), wt, wt,
            v_((L, 768), f32), v_((L, 128), f32), v_((L, 768), bf16), v_((4, L, 768), bf16), v_((4, L, 768), bf16), v_((L, 768), f32),
            v_((L, 768), bf16), v_((768, L), bf16), v_((768, L), bf16), v_((4, 256, 768), bf16), v_((2, 2, 768, 768), bf16),
            dma((9,)), dma((2, 2)),
        ],
        compiler_params=pltpu.CompilerParams(vmem_limit_bytes=67043328),
    )(xs, cs, heads, g, vec)


def norm_stats(r):
    center = r - jnp.mean(r, axis=-1, keepdims=True)
    inv = lax.rsqrt(jnp.mean(center * center, axis=-1, keepdims=True) + EPSILON)
    return center * inv, inv


def norm_back(cot, gain, xhat, inv):
    e = cot * gain
    grad = (e - jnp.mean(e, -1, keepdims=True) - xhat * jnp.mean(e * xhat, -1, keepdims=True)) * inv
    return grad, jnp.sum(cot * xhat, 0), jnp.sum(cot, 0)


def middle(x, cot, heads, w1, w2, w3, bias_o, bias_h, bias_d, shift1, shift2, gain1, gain2):
    ein = functools.partial(jnp.einsum, preferred_element_type=f32)
    hid = x.astype(f32)
    resid1 = hid + ein("tpw,tdw->pd", heads, w1[:, :, 512:]) + bias_o
    xhat1, inv1 = norm_stats(resid1)
    normed = xhat1 * gain1 + shift1
    low = normed.astype(bf16)
    pre = ein("pd,tdf->tpf", low, w2) + bias_h[:, None, :]
    act, gelu_back = jax.vjp(lambda v: jax.nn.gelu(v, approximate=False), pre)
    act = act.astype(bf16)
    resid2 = normed + ein("tpf,tdf->pd", act, w3) + bias_d
    xhat2, inv2 = norm_stats(resid2)
    out = (xhat2 * gain2 + shift2).astype(bf16)
    g2, dgain2, dshift2 = norm_back(cot.astype(f32), gain2, xhat2, inv2)
    g2low = g2.astype(bf16)
    d3 = ein("pd,tpf->tdf", g2low, act).astype(bf16)
    gpre = gelu_back(ein("pd,tdf->tpf", g2low, w3))[0].astype(bf16)
    d2 = ein("pd,tpf->tdf", low, gpre).astype(bf16)
    gn = g2 + ein("tpf,tdf->pd", gpre, w2)
    g1, dgain1, dshift1 = norm_back(gn, gain1, xhat1, inv1)
    g1low = g1.astype(bf16)
    dout = ein("pd,tpw->tdw", g1low, heads).astype(bf16)
    dbh = jnp.sum(gpre, 1, dtype=f32)
    return out, g1, g1low, dout, d2, d3, (dgain1, dgain2, dshift1, dshift2, jnp.sum(g1, 0), dbh, jnp.sum(g2, 0))


def on_device(hidden_in, cotangent, prefix, w_qkv, w_out, w_in, w_down, biases, gains):
    rows = w_qkv.shape[0]
    n_t = lax.axis_size("tensor")
    t_me, d_me = lax.axis_index("tensor"), lax.axis_index("dp")
    n_dev = n_t * lax.axis_size("dp")
    s = jnp.stack([jnp.concatenate([w_qkv.reshape(rows, -1), w_out.T], axis=1), w_in, w_down.T])
    vecs = jnp.concatenate([biases, gains], 0)
    width = vecs.shape[1]
    vecs = jnp.pad(vecs, ((0, 4), (0, 128 - width)))
    seqs = lambda a: jnp.transpose(a, (1, 0, 2))
    h, c = seqs(hidden_in), seqs(cotangent)
    my_prefix = lax.dynamic_slice_in_dim(prefix, t_me, 1, 0)
    if lax.axis_size("dp") == 8:
        g, xs, cs, vec, proj, projT, heads, ot, lse = front(my_prefix, s, h, c, vecs)
        out4, g1, g1low, doutw, d, v = mid(xs, cs, heads, g, vec)
        gs, vs, oo, xx = back(my_prefix, xs, g1low, g1, g, proj, projT, ot, lse, doutw, d.reshape(2, 2, 2, 4, 2, rows, 768), v, out4)
        qv = vs[16:24, :256].reshape(4, 2, 256)
        vs = jnp.concatenate([qv[:, 0, :192].reshape(1, 768), qv[:, 1, :192].reshape(1, 768), vs[2:16]])
    else:
        ein = functools.partial(jnp.einsum, preferred_element_type=f32)
        g = lax.all_gather(lax.all_gather(s, "dp", axis=1, tiled=True), "tensor", axis=1)
        x = lax.all_to_all(h, "tensor", 0, 0, tiled=True).reshape(1024, 768)
        cot = lax.all_to_all(c, "tensor", 0, 0, tiled=True).reshape(1024, 768)
        b = lax.all_gather(vecs, ("dp", "tensor"), axis=0)
        w1, w2, w3 = [a.reshape(n_t, 768, 768) for a in g]
        vec = b.reshape(n_dev, 16, 128)[:, :12, :width].transpose(1, 0, 2).reshape(12, 768)
        bqkv = jnp.pad(jnp.stack([vec[0].reshape(4, 192), jnp.zeros((4, 192), f32), vec[1].reshape(4, 192)], 1).reshape(4, 1, 576), ((0, 0), (0, 0), (0, 64)))
        proj, projT, heads, ot, lse = attn_fwd(my_prefix, x, w1, bqkv)
        out, g1, g1low, doutw, d2, d3, small = middle(
            x, cot, heads, w1, w2, w3, vec[2], vec[3:7].reshape(4, 768), vec[7], vec[8], vec[9], vec[10], vec[11]
        )
        dgain1, dgain2, dshift1, dshift2, dbo, dbh, dbd = small
        gproj = attn_bwd(my_prefix, g1low, w1, proj, projT, ot, lse)
        gp = gproj[:, :, :576]
        dqkv = ein("pd,tpc->tdc", x, gp).astype(bf16)
        x4 = (g1 + ein("tpc,tdc->pd", gp, w1[:, :, :576])).astype(bf16).reshape(4, 256, 768)
        dbq = jnp.sum(gp[:, :, :192], 1, dtype=f32).reshape(1, 768)
        dbv = jnp.sum(gp[:, :, 384:], 1, dtype=f32).reshape(1, 768)
        d = jnp.stack([jnp.concatenate([dqkv, doutw[:, :, 64:]], 2), d2, d3])
        part = lax.all_to_all(d, "tensor", 1, 1, tiled=True).astype(f32).sum(1)
        part = part.astype(bf16).reshape(3, -1, rows, 768)
        gs = lax.all_to_all(part, "dp", 1, 1, tiled=True).astype(f32).sum(1)
        vs = lax.psum(
            jnp.concatenate([dbq, dbv, dbo[None], dbh, jnp.stack([dbd, dshift1, dshift2, dgain1, dgain2]), jnp.zeros((4, 768), f32)]),
            ("dp", "tensor"),
        )
        oo = lax.all_to_all(out.reshape(4, 256, 768), "tensor", 0, 0, tiled=True)
        xx = lax.all_to_all(x4, "tensor", 0, 0, tiled=True)
    mine = lax.dynamic_slice_in_dim(vs, (d_me * n_t + t_me) * width, width, 1)
    return (
        seqs(oo),
        seqs(xx),
        gs[0, :, :576].reshape(rows, 3, 192),
        gs[0, :, 576:].T,
        gs[1],
        gs[2].T,
        mine[:10],
        mine[10:12],
    )


def solution(mesh):
    placed = (
        P("tensor", "dp", None),
        P("tensor", "dp", None),
        P("dp"),
        P("dp", None, "tensor"),
        P("tensor", "dp"),
        P("dp", "tensor"),
        P("tensor", "dp"),
        P(None, ("dp", "tensor")),
        P(None, ("dp", "tensor")),
    )
    return jax.shard_map(on_device, mesh=mesh, in_specs=placed, out_specs=placed[:2] + placed[3:], check_vma=False)
```

profile of v0, /device:TPU:0, one launch (start us, length us, event | category | flops | bytes accessed | tf_op | source)
XLA Modules:
  0.0 312.8 jit_solution(16691068524798280257)
XLA Ops:
  0.6 0.0 copy-start.1
  0.7 1.4 dynamic_slice.6.prefix_ref
  2.0 1.3 select_maximum_fusion.b_ref
  3.3 0.9 copy.28
  4.2 1.1 copy.27
  5.3 0.2 copy.29
  5.5 0.1 maximum_bitcast_fusion
  5.5 1.8 pad_maximum_fusion.s_ref
  7.3 0.0 copy-done.1
  7.4 3.5 %copy_bitcast_fusion = (bf16[4,256,768]{2,1,0:T(8,128)(2,1)}, bf16[4,256,768]{2,1,0:T(8,128)(2,1)}) fusion(bf16[256,4,768]{2,1,0:T(4,128)(2,1)S(1)} %copy-done.1, bf16[256,4,768]{2,1,0:T(4,128)(2,1)} %param.9), kind=kLoop, calls=%fused_computation | loop fusion | bytes 6291456 | tf_op jit(solution)/shard_map/transpose | solution.py:833
  10.8 129.1 %shard_map.152 = (bf16[3,2,2,4,2,96,768]{6,5,4,3,2,1,0:T(8,128)(2,1)}, bf16[4,256,768]{2,1,0:T(8,128)(2,1)}, bf16[4,256,768]{2,1,0:T(8,128)(2,1)}, f32[16,768]{1...) custom-call(s32[1]{0:T(128)} %dynamic_slice.6.prefix_ref, ...), custom_call_target="tpu_custom_call" | custom-call | tf_op jit(solution)/shard_map/pallas_call | solution.py:610
  139.9 55.8 %shard_map.153 = (bf16[4,256,768]{2,1,0:T(8,128)(2,1)}, f32[1024,768]{1,0:T(8,128)}, bf16[1024,768]{1,0:T(8,128)(2,1)}, bf16[4,768,256]{2,1,0:T(8,128)(2,1)}, bf...) custom-call(bf16[4,256,768]{2,1,0:T(8,128)(2,1)} %get-tuple-element.27.x_ref, ...), custom_call_target="tpu_custom_call" | custom-call | tf_op jit(solution)/shard_map/pallas_call | solution.py:771
  195.7 107.3 %shard_map.154 = (f32[3,96,768]{2,1,0:T(8,128)}, f32[24,768]{1,0:T(8,128)}, bf16[4,256,768]{2,1,0:T(8,128)(2,1)}, bf16[4,256,768]{2,1,0:T(8,128)(2,1)}) custom-call(s32[1]{0:T(128)} %dynamic_slice.6.prefix_ref, bf16[4,256,768]{2,1,0:T(8,128)(2,1)} %get-tuple-element.27.x_ref, bf16[1024,768]{1,0:T(8,128)(2,1)} %get-tuple-element.32.g_ref, ...), custom_call_target="tpu_custom_call" | custom-call | tf_op jit(solution)/shard_map/pallas_call | solution.py:388
  303.0 0.0 copy-start
  303.0 3.9 %copy.35 = bf16[256,4,768]{2,1,0:T(4,128)(2,1)} copy(bf16[256,4,768]{2,0,1:T(8,128)(2,1)} %bitcast.29) | data formatting | bytes 3145728
  306.9 0.0 copy-done
  306.9 0.0 copy-start.3
  306.9 0.0 copy-start.2
  306.9 2.4 copy.36
  309.2 0.0 copy-done.3
  309.3 0.1 reshape_squeeze.11
  309.4 0.1 reshape_squeeze.10
  309.5 0.1 fusion.1
  309.5 0.0 copy-start.4
  309.5 0.6 slice.43
  310.1 0.0 copy-done.2
  310.1 0.1 slice_bitcast_fusion.2
  310.2 0.7 copy.38
  311.0 0.8 slice_bitcast_fusion
  311.8 0.1 copy.32
  312.0 0.9 copy.37
  312.8 0.0 copy-done.4
  (5 shorter events, 0.1 us)
Async XLA Ops:
  0.6 6.7 %copy-start.1 = (bf16[256,4,768]{2,1,0:T(4,128)(2,1)S(1)}, bf16[256,4,768]{2,1,0:T(4,128)(2,1)}, u32[]{:S(2)}) copy-start(bf16[256,4,768]{2,1,0:T(4,128)(2,1)} %param.10) | copy-start | bytes 4718596
  303.0 3.9 %copy-start = (bf16[4,256,768]{2,1,0:T(8,128)(2,1)S(1)}, bf16[4,256,768]{2,1,0:T(8,128)(2,1)}, u32[]{:S(2)}) copy-start(bf16[4,256,768]{2,1,0:T(8,128)(2,1)} %get-tuple-element.43) | copy-start | bytes 4718596
  306.9 2.4 copy-start.3
  306.9 3.2 %copy-start.2 = (f32[3,96,768]{2,1,0:T(8,128)S(1)}, f32[3,96,768]{2,1,0:T(8,128)}, u32[]{:S(2)}) copy-start(f32[3,96,768]{2,1,0:T(8,128)} %get-tuple-element.44) | copy-start | bytes 2654212
  309.5 3.3 %copy-start.4 = (f32[16,24]{1,0:T(8,128)}, f32[16,24]{1,0:T(8,128)S(1)}, u32[]{:S(2)}) copy-start(f32[16,24]{1,0:T(8,128)S(1)} %fusion.1) | copy-start | bytes 4612
where the time goes:
time: 313 us
  Pallas kernels  292 us (93%)
  local copies, waits for them, and re-layouts  16.7 us (5%)
  other arithmetic  3.29 us (1%)
    pallas_call x1, Pallas kernels, front(): pl.pallas_call(front_kernel, out_shape=[sd((3, 2, 2, 4, 2, 96, 768), bf16...  129 us
    pallas_call x1, Pallas kernels, back(): pl.pallas_call(back_kernel, out_shape=[sd((3, 96, 768), f32), sd((24, 768...  107 us
    pallas_call x1, Pallas kernels, mid(): pl.pallas_call(mid_kernel, out_shape=[sd((4, 256, 768), bf16), sd((L, 768...  55.8 us
    unnamed x16, local copies, waits for them, and re-layouts  9.84 us

commit v1 on v0

--- a/solution.py
+++ b/solution.py
@@ -459,74 +459,132 @@
             k.wait_send()
 
 
-N_A = 6 * 11 + 6
+class Slabs:
+    def __init__(self, pc, src, dst, kind, rows, sems):
+        src = src.at[rows]
+        at = lambda y, z, x: dst.at[y, pc.c, z, x, rows]
+        every = slice(None)
+        mine, other = pc.y, 1 - pc.y
+        self.copy, self.fwd = {}, {}
+
+        def add(name, dim, pairs, got):
+            self.copy[name] = [rcopy(a, b, sems, pc.peer(dim, j)) for j, a, b in pairs]
+            if got is not None:
+                self.fwd[name] = rcopy(got, got, sems, pc.peer("c"))
+
+        slab = at(mine, every, pc.x)
+        add("z", "z", [(j, src, at(mine, pc.z, pc.x)) for j in (3, 2, 1)], slab)
+        add("x", "x", [(1, slab, slab)], at(mine, every, 1 - pc.x))
+        if kind == "A":
+            whole = at(mine, every, every)
+            add("y", "y", [(1, whole, whole)], at(other, every, every))
+        else:
+            add("y", "y", [(1, src, at(mine, pc.z, pc.x))], None)
+            one, slab2 = at(other, pc.z, pc.x), at(other, every, pc.x)
+            add("z2", "z", [(j, one, one) for j in (3, 2, 1)], slab2)
+            add("x2", "x", [(1, slab2, slab2)], at(other, every, 1 - pc.x))
+
+    def start(self, name):
+        for k in self.copy[name]:
+            k.start()
+
+    def arrive(self, name):
+        for k in self.copy[name]:
+            k.wait_recv()
+        if name in self.fwd:
+            self.fwd[name].start()
+
+    def from_core(self, *names):
+        for n in names:
+            self.fwd[n].wait_recv()
+
+    def end(self):
+        for ks in self.copy.values():
+            for k in ks:
+                k.wait_send()
+        for k in self.fwd.values():
+            k.wait_send()
+
+
+N_A = 3 * 8 + 3 * 13 + 11 + 3
 
 
 def front_kernel(
-    prefix_ref, s_ref, h_ref, c_ref, b_ref,
-    g_ref, x_ref, co_ref, vec_ref, proj_ref, projT_ref, heads_ref, ot_ref, lse_ref,
-    bv, sv, xv, cst, wv, proj_b, projT_b, heads_b, ot_b, lse_b, zq, mask_ref, ss, rs, ls, os_,
+    prefix_ref, s_ref, h_ref, b_ref,
+    g_ref, x_ref, vec_ref, proj_ref, projT_ref, heads_ref, ot_ref, lse_ref,
+    bv, sv, xv, wv, proj_b, projT_b, heads_b, ot_b, lse_b, zq, mask_ref, ss, rs, ls, os_,
 ):
     pc = Place()
     sems = Sems(ss, rs)
     own = (pc.y, pc.c, pc.z, pc.x)
     l_s = local(s_ref, sv, ls.at[0])
     l_h = local(h_ref.at[pc.t], xv.at[pc.t], ls.at[1])
-    l_c = local(c_ref.at[pc.t], cst, ls.at[2])
     l_b = local(b_ref, bv.at[own], ls.at[9])
     barrier(pc.peers_all())
     bias = Gather(pc, b_ref, bv, None, "zxy", sems)
-    w1 = Gather(pc, s_ref.at[0], g_ref.at[0], None, "zxy", sems)
-    w2 = [Gather(pc, s_ref.at[1], g_ref.at[1], (48 * i, 48), "yzx", sems) for i in range(2)]
-    w3 = [Gather(pc, s_ref.at[2], g_ref.at[2], (48 * i, 48), "yzx", sems) for i in range(2)]
+    w1a, w1b, w2a, w2b, w3a, w3b = every = [
+        Slabs(pc, s_ref.at[n // 2], g_ref.at[n // 2], kind, pl.ds(48 * (n % 2), 48), sems) for n, kind in enumerate("ABAABB")
+    ]
     bias.start()
-    w1.start()
-    w2[0].start()
-    w2[1].start()
+    w1b.start("y")
+    w1a.start("z")
+    w1b.start("z")
     hx = exchange(pc, h_ref, xv, sems)
-    w3[0].start()
-    w3[1].start()
+    w3a.start("y")
+    w3b.start("y")
     l_s.wait()
     l_g = [local(sv.at[g], g_ref.at[g].at[own], ls.at[3 + g]) for g in range(3)]
-    l_c.wait()
-    l_c2 = local(cst, co_ref.at[pc.t], ls.at[6])
     masks(mask_ref, prefix_ref[0])
     zq[...] = jnp.zeros_like(zq)
     ot_b[...] = jnp.zeros_like(ot_b)
     for q in l_g:
         q.wait()
     l_b.wait()
-    w1.next(1)
+    w1b.arrive("y")
+    w1b.start("z2")
+    for g in (w2a, w2b, w3a):
+        g.start("z")
     bias.next(1)
-    w2[0].next(1)
-    w1.next(2)
+    w1a.arrive("z")
+    w1a.start("x")
     bias.next(2)
-    w2[1].next(1)
+    w1b.arrive("z")
+    w1b.start("x")
+    w1a.arrive("x")
+    w1a.start("y")
+    w1b.arrive("z2")
+    w1b.start("x2")
+    w1b.arrive("x")
     bias.arrive(2)
     bias.from_core(0, len(bias.core))
     l_h.wait()
     for q in hx:
         q.wait_recv()
     l_x = local(xv, x_ref, ls.at[7])
-    c_plan = [rcopy(c_ref.at[pc.t ^ j], co_ref.at[pc.t], sems, (pc.dp, pc.t ^ j)) for j in (2, 3, 1)]
 
     def load(k, slot):
         t = pc.t ^ k
         return pltpu.make_async_copy(g_ref.at[0, t // 2, t % 2], wv.at[slot], ls.at[8])
 
-    def start_cot():
-        for q in c_plan:
-            q.start()
+    def go(g, got, then=None, then_g=None):
+        def step():
+            g.arrive(got)
+            if then:
+                (then_g or g).start(then)
+        return step
 
     steps = {
-        (0, 1): [lambda: w3[0].next(1), lambda: w3[1].next(1)],
-        (0, 2): [lambda: w1.from_core(0, 5), lambda: load(1, 1).start()],
-        (1, 0): [lambda: w2[0].next(2)],
-        (1, 1): [start_cot],
-        (1, 3): [lambda: w1.arrive(2), lambda: load(2, 0).start()],
-        (2, 0): [lambda: w2[1].next(2)],
-        (2, 2): [lambda: w1.from_core(5, 6), lambda: load(3, 1).start()],
-        (3, 2): [lambda: w3[0].next(2)],
+        (0, 0): [go(w3a, "y", "z2"), lambda: w3b.start("z"), go(w3b, "y", "z2")],
+        (0, 2): [go(w2a, "z", "x"), lambda: w1a.from_core("z", "x"), lambda: w1b.from_core("z", "x"), lambda: load(1, 1).start()],
+        (0, 3): [go(w1b, "x2")],
+        (1, 1): [go(w2b, "z", "x")],
+        (1, 2): [go(w2a, "x", "y")],
+        (1, 3): [go(w1a, "y"), lambda: load(2, 0).start()],
+        (2, 1): [go(w3a, "z", "x"), go(w2b, "x", "y")],
+        (2, 2): [lambda: w1a.from_core("y"), lambda: w1b.from_core("z2", "x2"), lambda: load(3, 1).start()],
+        (3, 0): [go(w3a, "z2", "x2")],
+        (3, 1): [go(w3a, "x"), go(w2a, "y")],
+        (3, 3): [go(w3b, "z", "x")],
     }
     load(0, 0).start()
 
@@ -574,7 +632,9 @@
         return 0
 
     lax.fori_loop(0, 4, group, 0)
-    w3[1].next(2)
+    w3a.arrive("x2")
+    w3b.arrive("z2")
+    w3b.start("x2")
     tiles = [jnp.zeros((16, 128), f32) for _ in range(6)]
     lane = lax.broadcasted_iota(jnp.int32, (1, 128), 1)
     for i in range(32):
@@ -586,43 +646,44 @@
             tiles[j + 1] = tiles[j + 1] + jnp.where(lane < r, piece, 0.0)
     for j in range(6):
         vec_ref[:, 128 * j : 128 * j + 128] = tiles[j]
-    for g in w2 + w3:
-        g.arrive(2)
-    for g in w2 + w3:
-        g.from_core(0, 6)
+    w2b.arrive("y")
+    w3b.arrive("x")
+    w3b.arrive("x2")
+    for g in (w2a, w2b):
+        g.from_core("z", "x", "y")
+    for g in (w3a, w3b):
+        g.from_core("z", "x", "z2", "x2")
     for q in hx:
         q.wait_send()
-    for q in c_plan:
-        q.wait()
     l_x.wait()
-    l_c2.wait()
     for k in (2, 3):
         for q in outs(k, k % 2):
             q.wait()
-    for g in [bias, w1] + w2 + w3:
+    bias.end()
+    for g in every:
         g.end()
 
 
-def front(prefix, s, h, c, b):
+def front(prefix, s, h, b):
     v_ = pltpu.VMEM
     dma = pltpu.SemaphoreType.DMA
     sd = jax.ShapeDtypeStruct
     return pl.pallas_call(
         front_kernel,
         out_shape=[
-            sd((3, 2, 2, 4, 2, 96, 768), bf16), sd((4, 256, 768), bf16), sd((4, 256, 768), bf16), sd((16, 768), f32),
+            sd((3, 2, 2, 4, 2, 96, 768), bf16), sd((4, 256, 768), bf16), sd((16, 768), f32),
             sd((4, L, 640), bf16), sd((4, 640, L), bf16), sd((4, L, 256), bf16), sd((4, 256, L), bf16), sd((4, 8, L), f32),
         ],
-        in_specs=[pl.BlockSpec(memory_space=pltpu.SMEM)] + [HBM] * 3 + [VM],
-        out_specs=[HBM] * 3 + [VM] + [HBM] * 5,
+        in_specs=[pl.BlockSpec(memory_space=pltpu.SMEM)] + [HBM] * 2 + [VM],
+        out_specs=[HBM] * 2 + [VM] + [HBM] * 5,
         scratch_shapes=[
-            v_((2, 2, 4, 2, 16, 128), f32), v_((3, 96, 768), bf16), v_((4, 256, 768), bf16), v_((256, 768), bf16), v_((2, 4, 2, 96, 768), bf16),
+            v_((2, 2, 4, 2, 16, 128), f32), v_((3, 96, 768), bf16), v_((4, 256, 768), bf16), v_((2, 4, 2, 96, 768), bf16),
             v_((2, L, 640), bf16), v_((2, 640, L), bf16), v_((2, L, 256), bf16), v_((2, 256, L), bf16), v_((2, 8, L), f32),
             v_((3, 256, L), bf16), v_((4, 256, 256), f32),
             dma((N_A,)), dma((N_A,)), dma((10,)), dma((2, 5)),
         ],
         compiler_params=pltpu.CompilerParams(collective_id=0, has_side_effects=True, vmem_limit_bytes=67043328),
-    )(prefix, s, h, c, b)
+    )(prefix, s, h, b)
 
 
 EPSILON = 1e-12
@@ -641,14 +702,18 @@
 def mid_kernel(
     x_ref, c_ref, heads_ref, g_ref, vec_ref,
     out_ref, g1_ref, g1low_ref, dout_ref, d_ref, v_ref,
-    xv, cv, hv, wo, w2, w3, xhat, inv, low, act, gd, acc, glow, lowT, gT, stage, dst, ls, ds_,
+    xv, cv, hv, wo, w2, w3, xhat, inv, low, act, gd, acc, glow, lowT, gT, stage, dst, ls, ds_, ss, rs,
 ):
+    pc = Place()
+    sems = Sems(ss, rs)
     l_x = local(x_ref, xv, ls.at[0])
     l_h = local(heads_ref, hv, ls.at[1])
     l_wo = [local(g_ref.at[0, y, c, :, :, :, pl.ds(512, 256)], wo.at[2 * y + c], ls.at[2 + 2 * y + c]) for y in range(2) for c in range(2)]
     l_w2 = local(g_ref.at[1], w2, ls.at[6])
     l_w3 = local(g_ref.at[2], w3, ls.at[7])
-    l_c = local(c_ref, cv, ls.at[8])
+    l_c = local(c_ref.at[pc.t], cv.at[pc.t], ls.at[8])
+    barrier([(pc.dp, pc.t ^ j) for j in (1, 2, 3)])
+    cx = exchange(pc, c_ref, cv, sems)
     row = lambda n: vec_ref[n : n + 1, :]
     v_ref[...] = jnp.zeros_like(v_ref)
 
@@ -690,6 +755,8 @@
 
     lax.fori_loop(0, 16, up, 0)
     l_c.wait()
+    for q in cx:
+        q.wait()
 
     def second(b, _):
         rows = pl.ds(pl.multiple_of(b * 256, 256), 256)
@@ -777,9 +844,9 @@
             v_((4, 256, 768), bf16), v_((4, 256, 768), bf16), v_((4, L, 256), bf16), v_((4, 4, 2, 96, 256), bf16), wt, wt,
             v_((L, 768), f32), v_((L, 128), f32), v_((L, 768), bf16), v_((4, L, 768), bf16), v_((4, L, 768), bf16), v_((L, 768), f32),
             v_((L, 768), bf16), v_((768, L), bf16), v_((768, L), bf16), v_((4, 256, 768), bf16), v_((2, 2, 768, 768), bf16),
-            dma((9,)), dma((2, 2)),
+            dma((9,)), dma((2, 2)), dma((3,)), dma((3,)),
         ],
-        compiler_params=pltpu.CompilerParams(vmem_limit_bytes=67043328),
+        compiler_params=pltpu.CompilerParams(collective_id=2, has_side_effects=True, vmem_limit_bytes=67043328),
     )(xs, cs, heads, g, vec)
 
 
@@ -834,8 +901,8 @@
     h, c = seqs(hidden_in), seqs(cotangent)
     my_prefix = lax.dynamic_slice_in_dim(prefix, t_me, 1, 0)
     if lax.axis_size("dp") == 8:
-        g, xs, cs, vec, proj, projT, heads, ot, lse = front(my_prefix, s, h, c, vecs)
-        out4, g1, g1low, doutw, d, v = mid(xs, cs, heads, g, vec)
+        g, xs, vec, proj, projT, heads, ot, lse = front(my_prefix, s, h, vecs)
+        out4, g1, g1low, doutw, d, v = mid(xs, c, heads, g, vec)
         gs, vs, oo, xx = back(my_prefix, xs, g1low, g1, g, proj, projT, ot, lse, doutw, d.reshape(2, 2, 2, 4, 2, rows, 768), v, out4)
         qv = vs[16:24, :256].reshape(4, 2, 256)
         vs = jnp.concatenate([qv[:, 0, :192].reshape(1, 768), qv[:, 1, :192].reshape(1, 768), vs[2:16]])

time: 313 us -> 276 us (0.88)
  Pallas kernels: 292 us -> 255 us
    pallas_call x1, Pallas kernels: 129 us -> 94.9 us  [front(): pl.pallas_call(front_kernel, out_shape=[sd((3, 2, 2, 4, 2, 96, 768), bf16...]
    transpose x1 -> x0, local copies, waits for them, and re-layouts: 3.47 us -> none  [on_device(): seqs = lambda a: jnp.transpose(a, (1, 0, 2))]
    unnamed x16 -> x20, local copies, waits for them, and re-layouts: 9.84 us -> 13.2 us
where the time goes in v1:
time: 276 us
  Pallas kernels  255 us (92%)
  local copies, waits for them, and re-layouts  16.6 us (6%)
  other arithmetic  3.29 us (1%)
    pallas_call x1, Pallas kernels, back(): pl.pallas_call(back_kernel, out_shape=[sd((3, 96, 768), f32), sd((24, 768...  105 us
    pallas_call x1, Pallas kernels, front(): pl.pallas_call(front_kernel, out_shape=[sd((3, 2, 2, 4, 2, 96, 768), bf16...  94.9 us
    pallas_call x1, Pallas kernels, mid(): pl.pallas_call(mid_kernel, out_shape=[sd((4, 256, 768), bf16), sd((L, 768...  55.8 us
    unnamed x20, local copies, waits for them, and re-layouts  13.2 us

profile of v1, /device:TPU:0, one launch (start us, length us, event | category | flops | bytes accessed | tf_op | source)
XLA Modules:
  0.0 275.8 jit_solution(15025852143345340323)
XLA Ops:
  0.6 0.0 copy-start
  0.6 1.4 dynamic_slice.6.prefix_ref
  2.0 1.3 select_maximum_fusion.b_ref
  3.3 0.9 copy.28
  4.2 1.1 copy.27
  5.3 0.2 copy.29
  5.4 0.1 maximum_bitcast_fusion
  5.5 1.8 pad_maximum_fusion.s_ref
  7.3 0.0 copy-done
  7.4 0.0 copy-start.1
  7.4 1.3 copy.44
  8.7 0.6 copy-done.1
  9.3 1.3 copy.43
  10.7 94.9 %shard_map.152 = (bf16[3,2,2,4,2,96,768]{6,5,4,3,2,1,0:T(8,128)(2,1)}, bf16[4,256,768]{2,1,0:T(8,128)(2,1)}, f32[16,768]{1,0:T(8,128)}, bf16[4,1024,640]{2,1,0:T...) custom-call(s32[1]{0:T(128)} %dynamic_slice.6.prefix_ref, ...), custom_call_target="tpu_custom_call" | custom-call | tf_op jit(solution)/shard_map/pallas_call | solution.py:671
  105.6 55.8 %shard_map.153 = (bf16[4,256,768]{2,1,0:T(8,128)(2,1)}, f32[1024,768]{1,0:T(8,128)}, bf16[1024,768]{1,0:T(8,128)(2,1)}, bf16[4,768,256]{2,1,0:T(8,128)(2,1)}, bf...) custom-call(bf16[4,256,768]{2,1,0:T(8,128)(2,1)} %get-tuple-element.26.x_ref, bf16[4,256,768]{2,1,0:T(8,128)(2,1)} %bitcast.31, ...), custom_call_target="tpu_custom_call" | custom-call | tf_op jit(solution)/shard_map/pallas_call | solution.py:838
  161.3 104.5 %shard_map.154 = (f32[3,96,768]{2,1,0:T(8,128)}, f32[24,768]{1,0:T(8,128)}, bf16[4,256,768]{2,1,0:T(8,128)(2,1)}, bf16[4,256,768]{2,1,0:T(8,128)(2,1)}) custom-call(s32[1]{0:T(128)} %dynamic_slice.6.prefix_ref, bf16[4,256,768]{2,1,0:T(8,128)(2,1)} %get-tuple-element.26.x_ref, bf16[1024,768]{1,0:T(8,128)(2,1)} %get-tuple-element.30.g_ref, ...), custom_call_target="tpu_custom_call" | custom-call | tf_op jit(solution)/shard_map/pallas_call | solution.py:388
  265.9 0.0 copy-start.2
  265.9 3.9 %copy.35 = bf16[256,4,768]{2,1,0:T(4,128)(2,1)} copy(bf16[256,4,768]{2,0,1:T(8,128)(2,1)} %bitcast.33) | data formatting | bytes 3145728
  269.8 0.0 copy-done.2
  269.8 0.0 copy-start.4
  269.8 0.0 copy-start.3
  269.8 2.4 copy.36
  272.1 0.0 copy-done.4
  272.2 0.1 reshape_squeeze.11
  272.3 0.1 reshape_squeeze.10
  272.4 0.1 fusion.1
  272.4 0.0 copy-start.5
  272.5 0.6 slice.43
  273.0 0.0 copy-done.3
  273.0 0.1 slice_bitcast_fusion.2
  273.1 0.7 copy.38
  273.9 0.8 slice_bitcast_fusion
  274.7 0.1 copy.32
  274.9 0.9 copy.37
  275.8 0.0 copy-done.5
  (5 shorter events, 0.1 us)
Async XLA Ops:
  0.6 6.7 %copy-start = (bf16[256,4,768]{2,1,0:T(4,128)(2,1)S(1)}, bf16[256,4,768]{2,1,0:T(4,128)(2,1)}, u32[]{:S(2)}) copy-start(bf16[256,4,768]{2,1,0:T(4,128)(2,1)} %param.9) | copy-start | bytes 4718596
  7.4 2.0 copy-start.1
  265.9 3.9 %copy-start.2 = (bf16[4,256,768]{2,1,0:T(8,128)(2,1)S(1)}, bf16[4,256,768]{2,1,0:T(8,128)(2,1)}, u32[]{:S(2)}) copy-start(bf16[4,256,768]{2,1,0:T(8,128)(2,1)} %get-tuple-element.41) | copy-start | bytes 4718596
  269.8 2.4 copy-start.4
  269.8 3.2 %copy-start.3 = (f32[3,96,768]{2,1,0:T(8,128)S(1)}, f32[3,96,768]{2,1,0:T(8,128)}, u32[]{:S(2)}) copy-start(f32[3,96,768]{2,1,0:T(8,128)} %get-tuple-element.42) | copy-start | bytes 2654212
  272.4 3.3 %copy-start.5 = (f32[16,24]{1,0:T(8,128)}, f32[16,24]{1,0:T(8,128)S(1)}, u32[]{:S(2)}) copy-start(f32[16,24]{1,0:T(8,128)S(1)} %fusion.1) | copy-start | bytes 4612

commit v2 on v1

--- a/solution.py
+++ b/solution.py
@@ -152,14 +152,19 @@
 
 
 class Reduce:
-    def __init__(self, pc, d_ref, half, lc, rc, r1, r2, r3, sems, lsem):
-        self.pc, self.lc, self.rc, self.r1, self.r2, self.r3 = pc, lc, rc, r1, r2, r3
+    def __init__(self, pc, kind, d_ref, half, lc, rc, r1, r2, r3, sems, lsem):
+        self.pc, self.kind, self.lc, self.rc, self.r1, self.r2, self.r3 = pc, kind, lc, rc, r1, r2, r3
         rows = pl.ds(48 * half, 48)
         self.own = pltpu.make_async_copy(d_ref.at[:, pc.c, :, :, rows], lc, lsem)
         self.q0 = rcopy(d_ref.at[:, 1 - pc.c, :, :, rows], rc, sems, pc.peer("c"))
-        self.q1 = rcopy(lc.at[:, :, 1 - pc.x], r1, sems, pc.peer("x"))
-        self.q2 = [rcopy(lc.at[:, pc.z ^ j, pc.x], r2.at[j - 1], sems, pc.peer("z", j)) for j in (3, 2, 1)]
-        self.q3 = rcopy(lc.at[1 - pc.y, pc.z, pc.x], r3, sems, pc.peer("y"))
+        if kind == "x":
+            self.q1 = rcopy(lc.at[:, :, 1 - pc.x], r1, sems, pc.peer("x"))
+            self.q2 = [rcopy(lc.at[:, pc.z ^ j, pc.x], r2.at[j - 1], sems, pc.peer("z", j)) for j in (3, 2, 1)]
+            self.q3 = [rcopy(lc.at[1 - pc.y, pc.z, pc.x], r3.at[0], sems, pc.peer("y"))]
+        else:
+            self.q1 = rcopy(lc.at[1 - pc.y], r1, sems, pc.peer("y"))
+            self.q2 = [rcopy(lc.at[pc.y, :, 1 - pc.x], r2, sems, pc.peer("x"))]
+            self.q3 = [rcopy(lc.at[pc.y, pc.z ^ j, pc.x], r3.at[j - 1], sems, pc.peer("z", j)) for j in (3, 2, 1)]
 
     def s0(self):
         self.own.start()
@@ -174,7 +179,10 @@
 
     def s2(self):
         self.q1.wait_recv()
-        add_into(self.lc, self.r1, 8, lambda j: (j // 4, j % 4, self.pc.x), lambda j: (j // 4, j % 4))
+        if self.kind == "x":
+            add_into(self.lc, self.r1, 8, lambda j: (j // 4, j % 4, self.pc.x), lambda j: (j // 4, j % 4))
+        else:
+            add_into(self.lc, self.r1, 8, lambda j: (self.pc.y, j // 2, j % 2), lambda j: (j // 2, j % 2))
         for q in self.q2:
             q.start()
 
@@ -182,31 +190,39 @@
         pc = self.pc
         for q in self.q2:
             q.wait_recv()
-        for y in range(2):
-            at = (y, pc.z, pc.x)
-            total = (self.lc[at].astype(f32) + self.r2[0, y].astype(f32)) + (self.r2[1, y].astype(f32) + self.r2[2, y].astype(f32))
-            self.lc[at] = total.astype(bf16)
-        self.q3.start()
+        if self.kind == "x":
+            for y in range(2):
+                at = (y, pc.z, pc.x)
+                total = (self.lc[at].astype(f32) + self.r2[0, y].astype(f32)) + (self.r2[1, y].astype(f32) + self.r2[2, y].astype(f32))
+                self.lc[at] = total.astype(bf16)
+        else:
+            add_into(self.lc, self.r2, 4, lambda j: (pc.y, j, pc.x), lambda j: (j,))
+        for q in self.q3:
+            q.start()
 
     def s4(self, out_ref, rows):
         pc = self.pc
-        self.q3.wait_recv()
-        out_ref[rows] = self.lc[pc.y, pc.z, pc.x].astype(f32) + self.r3[...].astype(f32)
+        for q in self.q3:
+            q.wait_recv()
+        total = self.lc[pc.y, pc.z, pc.x].astype(f32) + self.r3[0].astype(f32)
+        if self.kind == "y":
+            total = total + (self.r3[1].astype(f32) + self.r3[2].astype(f32))
+        out_ref[rows] = total
 
     def end(self):
-        for q in [self.q0, self.q1, self.q3] + self.q2:
+        for q in [self.q0, self.q1] + self.q2 + self.q3:
             q.wait_send()
 
 
-N_C = 4 * 6 + 1 + 1 + 1 + 2 + 6 + 6 + 6
+N_C = 4 * 6 + 3 + 3 + 8 + 6 + 6
 
 
 def back_kernel(
-    prefix_ref, x_ref, g_ref, gf_ref, w_ref, proj_ref, projT_ref, ot_ref, lse_ref, dout_ref, d_ref, v_ref, out_ref,
-    gs_ref, vs_ref, oo_ref, xo_ref,
+    prefix_ref, x_ref, g_ref, gf_ref, w_ref, proj_ref, projT_ref, ot_ref, lse_ref, dout_ref, d_ref, v_ref,
+    gs_ref, vs_ref, xo_ref,
     xT, gl, dxa, w_b, proj_b, projT_b, ot_b, lse_b, dout_b,
     zq, zdo, qm, dom, pt, ds, mask_ref, gt, dqt, dkb, dvb, gproj,
-    lc, rc, r1, r2, r3, dwb, cr, yr, xr, zr, vb, vr, xst, ss, rs, ls, ins,
+    lc, rc, yx1, yx2, yx3, yy1, yy2, yy3, dwb, cr, yr, xr, zr, vb, vr, xst, ss, rs, ls, ins,
 ):
     pc = Place()
     sems = Sems(ss, rs)
@@ -228,21 +244,30 @@
     l_g = local(g_ref, gl, ls.at[5])
     l_f = local(gf_ref, dxa, ls.at[6])
     barrier(pc.peers_all())
-    red = {}
-    for n, (g, i) in enumerate(((1, 0), (1, 1), (0, 0), (0, 1))):
-        red[n] = Reduce(pc, d_ref.at[g], i, lc.at[n], rc.at[n], r1.at[n], r2.at[n], r3.at[n], sems, ls.at[n])
+    red = []
+    for n, (kind, g, i) in enumerate((("y", 1, 0), ("x", 1, 1), ("y", 0, 0), ("x", 0, 1))):
+        r1, r2, r3 = [r.at[n // 2] for r in ((yy1, yy2, yy3) if kind == "y" else (yx1, yx2, yx3))]
+        red.append(Reduce(pc, kind, d_ref.at[g], i, lc.at[n], rc.at[n], r1, r2, r3, sems, ls.at[n]))
         red[n].s0()
-    ox = exchange(pc, out_ref, oo_ref, sems)
-    l_o = [local(out_ref.at[pc.t], oo_ref.at[pc.t], ls.at[7])]
     q_c0 = rcopy(dwb.at[0], cr.at[0], sems, pc.peer("c"))
     q_y = rcopy(dwb.at[1], yr, sems, pc.peer("y"))
     q_c1 = rcopy(dwb.at[2], cr.at[1], sems, pc.peer("c"))
     half = [pl.ds(48 * i, 48) for i in range(2)]
-    q_x = [rcopy(dwb.at[3, :, 1 - pc.x, half[i]], xr.at[i], sems, pc.peer("x")) for i in range(2)]
-    q_z = [[rcopy(dwb.at[3, pc.z ^ j, pc.x, half[i]], zr.at[i, j - 1], sems, pc.peer("z", j)) for j in (3, 2, 1)] for i in range(2)]
+    q_x = [rcopy(dwb.at[3, pc.z ^ j, 1 - pc.x, half[i]], xr.at[i, pc.z ^ j], sems, pc.peer("x")) for i in range(2) for j in (3, 2, 1, 0)]
+    q_z = [rcopy(dwb.at[3, pc.z ^ j, pc.x, half[i]], zr.at[i, j - 1], sems, pc.peer("z", j)) for i in range(2) for j in (3, 2, 1)]
+    v_q = [rcopy(vb.at[n], vr.at[n], sems, pc.peer(dim)) for n, dim in enumerate("cxy")]
+    v_z = [rcopy(vb.at[3], vr.at[2 + j], sems, pc.peer("z", j)) for j in (3, 2, 1)]
+
+    def vstep(n):
+        v_q[n].wait_recv()
+        vb[n + 1] = vb[n] + vr[n]
+        for q in [v_q[n + 1]] if n < 2 else v_z:
+            q.start()
+
     steps = {
-        (0, 1): [red[0].s1], (0, 2): [red[1].s1], (0, 3): [red[2].s1], (1, 1): [red[3].s1],
-        (1, 3): [red[0].s2], (2, 3): [red[1].s2], (3, 0): [red[0].s3], (3, 3): [red[2].s2],
+        (0, 0): [red[0].s1], (0, 1): [red[1].s1], (0, 2): [red[2].s1], (0, 3): [red[3].s1],
+        (1, 1): [red[1].s2], (1, 2): [red[0].s2], (2, 1): [red[3].s2, red[2].s2], (2, 2): [red[1].s3],
+        (3, 0): [red[0].s3], (3, 1): [red[3].s3], (3, 2): [red[2].s3],
     }
     masks(mask_ref, prefix_ref[0])
     zq[...] = jnp.zeros_like(zq)
@@ -297,6 +322,11 @@
         gproj[:, 384:576] = dvb[:, 64:256]
         vb[0, pl.ds(16 + 2 * t, 1), 0:256] = jnp.sum(gproj[:, 0:256].astype(f32), axis=0, keepdims=True)
         vb[0, pl.ds(17 + 2 * t, 1), 0:256] = jnp.sum(gproj[:, 384:640].astype(f32), axis=0, keepdims=True)
+
+        @pl.when(k == 3)
+        def _():
+            v_q[0].start()
+
         dw = dotf(xT[...], gproj[...])
         do = dout_b[slot].astype(f32)
         shape = lambda a: a.astype(bf16).reshape(4, 2, 96, a.shape[1])
@@ -320,6 +350,7 @@
 
         @pl.when(k == 3)
         def _():
+            vstep(0)
             q_c1.wait_recv()
             add_into(dwb.at[3], cr.at[1], 8, lambda j: (j // 2, j % 2), lambda j: (j // 2, j % 2))
             q_y.wait_recv()
@@ -331,77 +362,67 @@
         return 0
 
     lax.fori_loop(0, 4, group, 0)
+    vstep(1)
     xst[...] = dxa[...].astype(bf16).reshape(4, 256, 768)
-    v_q = [rcopy(vb.at[0], vr.at[0], sems, pc.peer("c"))]
-    v_q[0].start()
     xx = exchange(pc, xst, xo_ref, sems)
-    l_o.append(local(xst.at[pc.t], xo_ref.at[pc.t], ls.at[8]))
-
-    def vstep(n, dim):
-        v_q[n].wait_recv()
-        vb[n + 1] = vb[n] + vr[n]
-        v_q.append(rcopy(vb.at[n + 1], vr.at[n + 1], sems, pc.peer(dim)))
-        v_q[n + 1].start()
-
-    vstep(0, "x")
-    red[1].s3()
-    for i in range(2):
-        q_x[i].wait_recv()
-        for z in range(4):
-            dwb[3, z, pc.x, half[i]] = (dwb[3, z, pc.x, half[i]].astype(f32) + xr[i, z].astype(f32)).astype(bf16)
-        for q in q_z[i]:
-            q.start()
-    vstep(1, "y")
-    red[3].s2()
-    red[2].s3()
-    v_q[2].wait_recv()
-    vb[3] = vb[2] + vr[2]
-    v_z = [rcopy(vb.at[3], vr.at[2 + j], sems, pc.peer("z", j)) for j in (3, 2, 1)]
-    for q in v_z:
-        q.start()
-    red[0].s4(gs_ref.at[2], slice(0, 48))
+    l_o = local(xst.at[pc.t], xo_ref.at[pc.t], ls.at[7])
+    vstep(2)
+
+    def arrive(n, j):
+        i, z = n // 4, pc.z ^ j
+        q_x[n].wait_recv()
+        dwb[3, z, pc.x, half[i]] = (dwb[3, z, pc.x, half[i]].astype(f32) + xr[i, z].astype(f32)).astype(bf16)
+
+    for n in range(8):
+        j = 3 - n % 4
+        arrive(n, j)
+        if j:
+            q_z[n - n // 4].start()
+        if n == 1:
+            red[0].s4(gs_ref.at[2], slice(0, 48))
+        if n == 3:
+            red[2].s4(gs_ref.at[1], slice(0, 48))
     red[1].s4(gs_ref.at[2], slice(48, 96))
-    red[3].s3()
-    for i in range(2):
-        for q in q_z[i]:
-            q.wait_recv()
-        gs_ref[0, 48 * i : 48 * i + 48] = (dwb[3, pc.z, pc.x, half[i]].astype(f32) + zr[i, 0].astype(f32)) + (zr[i, 1].astype(f32) + zr[i, 2].astype(f32))
-    red[2].s4(gs_ref.at[1], slice(0, 48))
+    red[3].s4(gs_ref.at[1], slice(48, 96))
     for q in v_z:
         q.wait_recv()
     vs_ref[...] = (vb[3] + vr[3]) + (vr[4] + vr[5])
-    red[3].s4(gs_ref.at[1], slice(48, 96))
-    for q in l_o:
+    for i in range(2):
+        for q in q_z[3 * i : 3 * i + 3]:
+            q.wait_recv()
+        gs_ref[0, 48 * i : 48 * i + 48] = (dwb[3, pc.z, pc.x, half[i]].astype(f32) + zr[i, 0].astype(f32)) + (zr[i, 1].astype(f32) + zr[i, 2].astype(f32))
+    l_o.wait()
+    for q in xx:
         q.wait()
-    for q in ox + xx:
-        q.wait()
-    for n in range(4):
-        red[n].end()
-    for q in [q_c0, q_y, q_c1] + q_x + q_z[0] + q_z[1] + v_q + v_z:
+    for r in red:
+        r.end()
+    for q in [q_c0, q_y, q_c1] + q_x + q_z + v_q + v_z:
         q.wait_send()
 
 
-def back(prefix, x, g1low, g1, g, proj, projT, ot, lse, doutw, d, v, out4):
+def back(prefix, x, g1low, g1, g, proj, projT, ot, lse, doutw, d, v):
     v_ = pltpu.VMEM
     dma = pltpu.SemaphoreType.DMA
     sd = jax.ShapeDtypeStruct
     return pl.pallas_call(
         back_kernel,
-        out_shape=[sd((3, 96, 768), f32), sd((24, 768), f32), sd((4, 256, 768), bf16), sd((4, 256, 768), bf16)],
-        in_specs=[pl.BlockSpec(memory_space=pltpu.SMEM)] + [HBM] * 10 + [VM, HBM],
-        out_specs=[VM, VM, HBM, HBM],
+        out_shape=[sd((3, 96, 768), f32), sd((24, 768), f32), sd((4, 256, 768), bf16)],
+        in_specs=[pl.BlockSpec(memory_space=pltpu.SMEM)] + [HBM] * 10 + [VM],
+        out_specs=[VM, VM, HBM],
         scratch_shapes=[
             v_((768, L), bf16), v_((L, 768), bf16), v_((L, 768), f32),
             v_((2, 4, 2, 96, 768), bf16), v_((2, L, 640), bf16), v_((2, 640, L), bf16), v_((2, 256, L), bf16), v_((2, 8, L), f32), v_((2, 768, 256), bf16),
             v_((3, 256, L), bf16), v_((3, 256, L), bf16), v_((L, 256), bf16), v_((L, 256), bf16), v_((L, L), bf16), v_((L, L), bf16),
             v_((4, 256, 256), f32), v_((256, L), bf16), v_((192, L), bf16), v_((L, 256), bf16), v_((L, 256), bf16), v_((L, 640), bf16),
-            v_((4, 2, 4, 2, 48, 768), bf16), v_((4, 2, 4, 2, 48, 768), bf16), v_((4, 2, 4, 48, 768), bf16), v_((4, 3, 2, 48, 768), bf16), v_((4, 48, 768), bf16),
+            v_((4, 2, 4, 2, 48, 768), bf16), v_((4, 2, 4, 2, 48, 768), bf16),
+            v_((2, 2, 4, 48, 768), bf16), v_((2, 3, 2, 48, 768), bf16), v_((2, 1, 48, 768), bf16),
+            v_((2, 4, 2, 48, 768), bf16), v_((2, 4, 48, 768), bf16), v_((2, 3, 48, 768), bf16),
             v_((4, 4, 2, 96, 768), bf16), v_((2, 4, 2, 96, 768), bf16), v_((4, 2, 96, 768), bf16), v_((2, 4, 48, 768), bf16), v_((2, 3, 48, 768), bf16),
             v_((4, 24, 768), f32), v_((6, 24, 768), f32), v_((4, 256, 768), bf16),
-            dma((N_C,)), dma((N_C,)), dma((9,)), dma((2, 6)),
+            dma((N_C,)), dma((N_C,)), dma((8,)), dma((2, 6)),
         ],
         compiler_params=pltpu.CompilerParams(collective_id=1, has_side_effects=True, vmem_limit_bytes=67043328),
-    )(prefix, x, g1low, g1, g, proj, projT, ot, lse, doutw, d, v, out4)
+    )(prefix, x, g1low, g1, g, proj, projT, ot, lse, doutw, d, v)
 
 
 class Gather:
@@ -701,7 +722,7 @@
 
 def mid_kernel(
     x_ref, c_ref, heads_ref, g_ref, vec_ref,
-    out_ref, g1_ref, g1low_ref, dout_ref, d_ref, v_ref,
+    oo_ref, g1_ref, g1low_ref, dout_ref, d_ref, v_ref,
     xv, cv, hv, wo, w2, w3, xhat, inv, low, act, gd, acc, glow, lowT, gT, stage, dst, ls, ds_, ss, rs,
 ):
     pc = Place()
@@ -776,7 +797,8 @@
         return 0
 
     lax.fori_loop(0, 4, second, 0)
-    l_o = local(stage, out_ref, ls.at[0])
+    ox = exchange(pc, stage, oo_ref, sems)
+    l_o = local(stage.at[pc.t], oo_ref.at[pc.t], ls.at[0])
     gT[...] = glow[...].T
     lowT[...] = low[...].T
 
@@ -826,7 +848,7 @@
     for t in range(4):
         dst[t // 2, t % 2, :, 0:256] = dotf(gT[...], hv[t]).astype(bf16)
     l_d = [local(dst.at[t // 2, t % 2, :, pl.ds(0, 256)], dout_ref.at[t], ls.at[3 + t]) for t in range(4)]
-    for q in [l_o] + l_g + l_d:
+    for q in [l_o] + l_g + l_d + ox:
         q.wait()
 
 
@@ -844,7 +866,7 @@
             v_((4, 256, 768), bf16), v_((4, 256, 768), bf16), v_((4, L, 256), bf16), v_((4, 4, 2, 96, 256), bf16), wt, wt,
             v_((L, 768), f32), v_((L, 128), f32), v_((L, 768), bf16), v_((4, L, 768), bf16), v_((4, L, 768), bf16), v_((L, 768), f32),
             v_((L, 768), bf16), v_((768, L), bf16), v_((768, L), bf16), v_((4, 256, 768), bf16), v_((2, 2, 768, 768), bf16),
-            dma((9,)), dma((2, 2)), dma((3,)), dma((3,)),
+            dma((9,)), dma((2, 2)), dma((6,)), dma((6,)),
         ],
         compiler_params=pltpu.CompilerParams(collective_id=2, has_side_effects=True, vmem_limit_bytes=67043328),
     )(xs, cs, heads, g, vec)
@@ -902,8 +924,8 @@
     my_prefix = lax.dynamic_slice_in_dim(prefix, t_me, 1, 0)
     if lax.axis_size("dp") == 8:
         g, xs, vec, proj, projT, heads, ot, lse = front(my_prefix, s, h, vecs)
-        out4, g1, g1low, doutw, d, v = mid(xs, c, heads, g, vec)
-        gs, vs, oo, xx = back(my_prefix, xs, g1low, g1, g, proj, projT, ot, lse, doutw, d.reshape(2, 2, 2, 4, 2, rows, 768), v, out4)
+        oo, g1, g1low, doutw, d, v = mid(xs, c, heads, g, vec)
+        gs, vs, xx = back(my_prefix, xs, g1low, g1, g, proj, projT, ot, lse, doutw, d.reshape(2, 2, 2, 4, 2, rows, 768), v)
         qv = vs[16:24, :256].reshape(4, 2, 256)
         vs = jnp.concatenate([qv[:, 0, :192].reshape(1, 768), qv[:, 1, :192].reshape(1, 768), vs[2:16]])
     else:

time: 276 us -> 259 us (0.938)
  Pallas kernels: 255 us -> 238 us
    pallas_call x1, Pallas kernels: 105 us -> 87.6 us  [back(): pl.pallas_call(back_kernel, out_shape=[sd((3, 96, 768), f32), sd((24, 768...]
where the time goes in v2:
time: 259 us
  Pallas kernels  238 us (92%)
  local copies, waits for them, and re-layouts  16.6 us (6%)
  other arithmetic  3.28 us (1%)
    pallas_call x1, Pallas kernels, front(): pl.pallas_call(front_kernel, out_shape=[sd((3, 2, 2, 4, 2, 96, 768), bf16...  94.9 us
    pallas_call x1, Pallas kernels, back(): pl.pallas_call(back_kernel, out_shape=[sd((3, 96, 768), f32), sd((24, 768...  87.6 us
    pallas_call x1, Pallas kernels, mid(): pl.pallas_call(mid_kernel, out_shape=[sd((4, 256, 768), bf16), sd((L, 768...  55.8 us
    unnamed x20, local copies, waits for them, and re-layouts  13.2 us

profile of v2, /device:TPU:0, one launch (start us, length us, event | category | flops | bytes accessed | tf_op | source)
XLA Modules:
  0.0 258.9 jit_solution(4651308613050154757)
XLA Ops:
  0.6 0.0 copy-start
  0.6 1.4 dynamic_slice.6.prefix_ref
  2.0 1.3 select_maximum_fusion.b_ref
  3.3 0.9 copy.28
  4.2 1.1 copy.27
  5.3 0.2 copy.29
  5.4 0.1 maximum_bitcast_fusion
  5.5 1.8 pad_maximum_fusion.s_ref
  7.3 0.0 copy-done
  7.3 0.0 copy-start.1
  7.3 1.3 copy.44
  8.7 0.6 copy-done.1
  9.3 1.3 copy.43
  10.7 94.9 %shard_map.152 = (bf16[3,2,2,4,2,96,768]{6,5,4,3,2,1,0:T(8,128)(2,1)}, bf16[4,256,768]{2,1,0:T(8,128)(2,1)}, f32[16,768]{1,0:T(8,128)}, bf16[4,1024,640]{2,1,0:T...) custom-call(s32[1]{0:T(128)} %dynamic_slice.6.prefix_ref, ...), custom_call_target="tpu_custom_call" | custom-call | tf_op jit(solution)/shard_map/pallas_call | solution.py:692
  105.5 55.8 %shard_map.153 = (bf16[4,256,768]{2,1,0:T(8,128)(2,1)}, f32[1024,768]{1,0:T(8,128)}, bf16[1024,768]{1,0:T(8,128)(2,1)}, bf16[4,768,256]{2,1,0:T(8,128)(2,1)}, bf...) custom-call(bf16[4,256,768]{2,1,0:T(8,128)(2,1)} %get-tuple-element.25.x_ref, bf16[4,256,768]{2,1,0:T(8,128)(2,1)} %bitcast.31, ...), custom_call_target="tpu_custom_call" | custom-call | tf_op jit(solution)/shard_map/pallas_call | solution.py:860
  161.4 87.6 %shard_map.154 = (f32[3,96,768]{2,1,0:T(8,128)}, f32[24,768]{1,0:T(8,128)}, bf16[4,256,768]{2,1,0:T(8,128)(2,1)}) custom-call(s32[1]{0:T(128)} %dynamic_slice.6.prefix_ref, bf16[4,256,768]{2,1,0:T(8,128)(2,1)} %get-tuple-element.25.x_ref, bf16[1024,768]{1,0:T(8,128)(2,1)} %get-tuple-element.30.g_ref, f32[1024,768]{1,0:T(8,128)} %get-tuple-element.31.gf_ref, ...), custom_call_target="tpu_custom_call" | custom-call | tf_op jit(solution)/shard_map/pallas_call | solution.py:407
  249.0 0.0 copy-start.2
  249.0 3.9 %copy.36 = bf16[256,4,768]{2,1,0:T(4,128)(2,1)} copy(bf16[256,4,768]{2,0,1:T(8,128)(2,1)} %bitcast.33) | data formatting | bytes 3145728
  252.9 0.0 copy-done.2
  252.9 0.0 copy-start.4
  252.9 0.0 copy-start.3
  252.9 2.4 copy.35
  255.2 0.0 copy-done.4
  255.3 0.1 reshape_squeeze.11
  255.4 0.1 reshape_squeeze.10
  255.5 0.1 fusion.1
  255.6 0.0 copy-start.5
  255.6 0.6 slice.43
  256.1 0.0 copy-done.3
  256.1 0.1 slice_bitcast_fusion.2
  256.2 0.7 copy.38
  257.0 0.8 slice_bitcast_fusion
  257.8 0.1 copy.32
  258.0 0.9 copy.37
  258.9 0.0 copy-done.5
  (5 shorter events, 0.1 us)
Async XLA Ops:
  0.6 6.7 %copy-start = (bf16[256,4,768]{2,1,0:T(4,128)(2,1)S(1)}, bf16[256,4,768]{2,1,0:T(4,128)(2,1)}, u32[]{:S(2)}) copy-start(bf16[256,4,768]{2,1,0:T(4,128)(2,1)} %param.9) | copy-start | bytes 4718596
  7.3 2.0 copy-start.1
  249.0 3.9 %copy-start.2 = (bf16[4,256,768]{2,1,0:T(8,128)(2,1)S(1)}, bf16[4,256,768]{2,1,0:T(8,128)(2,1)}, u32[]{:S(2)}) copy-start(bf16[4,256,768]{2,1,0:T(8,128)(2,1)} %get-tuple-element.29) | copy-start | bytes 4718596
  252.9 2.4 copy-start.4
  252.9 3.2 %copy-start.3 = (f32[3,96,768]{2,1,0:T(8,128)S(1)}, f32[3,96,768]{2,1,0:T(8,128)}, u32[]{:S(2)}) copy-start(f32[3,96,768]{2,1,0:T(8,128)} %get-tuple-element.40) | copy-start | bytes 2654212
  255.6 3.3 %copy-start.5 = (f32[16,24]{1,0:T(8,128)}, f32[16,24]{1,0:T(8,128)S(1)}, u32[]{:S(2)}) copy-start(f32[16,24]{1,0:T(8,128)S(1)} %fusion.1) | copy-start | bytes 4612

commit v3 on v2

--- a/solution.py
+++ b/solution.py
@@ -269,7 +269,7 @@
         (1, 1): [red[1].s2], (1, 2): [red[0].s2], (2, 1): [red[3].s2, red[2].s2], (2, 2): [red[1].s3],
         (3, 0): [red[0].s3], (3, 1): [red[3].s3], (3, 2): [red[2].s3],
     }
-    masks(mask_ref, prefix_ref[0])
+    masks(mask_ref, prefix_ref[pc.t])
     zq[...] = jnp.zeros_like(zq)
     zdo[...] = jnp.zeros_like(zdo)
     gproj[:, 576:640] = jnp.zeros((L, 64), bf16)
@@ -278,6 +278,9 @@
     xT[...] = xst[...].reshape(L, 768).T
     l_g.wait()
     l_f.wait()
+
+    def chip_sum(i, z, x):
+        return dwb[3, z, x, half[i]].astype(f32) + (cr[1, z, x, half[i]].astype(f32) + yr[z, x, half[i]].astype(f32))
 
     def group(k, _):
         slot = k % 2
@@ -352,10 +355,10 @@
         def _():
             vstep(0)
             q_c1.wait_recv()
-            add_into(dwb.at[3], cr.at[1], 8, lambda j: (j // 2, j % 2), lambda j: (j // 2, j % 2))
             q_y.wait_recv()
-            add_into(dwb.at[3], yr, 8, lambda j: (j // 2, j % 2), lambda j: (j // 2, j % 2))
-            for q in q_x:
+            for n, q in enumerate(q_x):
+                i, z, x = n // 4, pc.z ^ (3 - n % 4), 1 - pc.x
+                dwb[3, z, x, half[i]] = chip_sum(i, z, x).astype(bf16)
                 q.start()
 
         dxa[...] += dot_nt(gproj[...], w[...].reshape(768, 768)[:, 0:640])
@@ -371,7 +374,7 @@
     def arrive(n, j):
         i, z = n // 4, pc.z ^ j
         q_x[n].wait_recv()
-        dwb[3, z, pc.x, half[i]] = (dwb[3, z, pc.x, half[i]].astype(f32) + xr[i, z].astype(f32)).astype(bf16)
+        dwb[3, z, pc.x, half[i]] = (chip_sum(i, z, pc.x) + xr[i, z].astype(f32)).astype(bf16)
 
     for n in range(8):
         j = 3 - n % 4
@@ -495,11 +498,17 @@
 
         slab = at(mine, every, pc.x)
         add("z", "z", [(j, src, at(mine, pc.z, pc.x)) for j in (3, 2, 1)], slab)
-        add("x", "x", [(1, slab, slab)], at(mine, every, 1 - pc.x))
+        if kind in "AB":
+            add("x", "x", [(1, slab, slab)], at(mine, every, 1 - pc.x))
         if kind == "A":
             whole = at(mine, every, every)
             add("y", "y", [(1, whole, whole)], at(other, every, every))
-        else:
+        if kind in "CE":
+            add("y", "y", [(1, slab, slab)], at(other, every, pc.x))
+        if kind == "E":
+            whole = at(every, every, pc.x)
+            add("x", "x", [(1, whole, whole)], at(every, every, 1 - pc.x))
+        if kind == "B":
             add("y", "y", [(1, src, at(mine, pc.z, pc.x))], None)
             one, slab2 = at(other, pc.z, pc.x), at(other, every, pc.x)
             add("z2", "z", [(j, one, one) for j in (3, 2, 1)], slab2)
@@ -527,7 +536,7 @@
             k.wait_send()
 
 
-N_A = 3 * 8 + 3 * 13 + 11 + 3
+N_A = 3 * 8 + 2 * 13 + 6 + 11 + 3
 
 
 def front_kernel(
@@ -544,18 +553,18 @@
     barrier(pc.peers_all())
     bias = Gather(pc, b_ref, bv, None, "zxy", sems)
     w1a, w1b, w2a, w2b, w3a, w3b = every = [
-        Slabs(pc, s_ref.at[n // 2], g_ref.at[n // 2], kind, pl.ds(48 * (n % 2), 48), sems) for n, kind in enumerate("ABAABB")
+        Slabs(pc, s_ref.at[n // 2], g_ref.at[n // 2], kind, rows, sems)
+        for n, (kind, rows) in enumerate(zip("ABABCE", [pl.ds(0, 48), pl.ds(48, 48)] * 3))
     ]
     bias.start()
     w1b.start("y")
     w1a.start("z")
     w1b.start("z")
     hx = exchange(pc, h_ref, xv, sems)
-    w3a.start("y")
-    w3b.start("y")
+    w2b.start("y")
     l_s.wait()
     l_g = [local(sv.at[g], g_ref.at[g].at[own], ls.at[3 + g]) for g in range(3)]
-    masks(mask_ref, prefix_ref[0])
+    masks(mask_ref, prefix_ref[pc.t])
     zq[...] = jnp.zeros_like(zq)
     ot_b[...] = jnp.zeros_like(ot_b)
     for q in l_g:
@@ -563,8 +572,6 @@
     l_b.wait()
     w1b.arrive("y")
     w1b.start("z2")
-    for g in (w2a, w2b, w3a):
-        g.start("z")
     bias.next(1)
     w1a.arrive("z")
     w1a.start("x")
@@ -576,6 +583,8 @@
     w1b.arrive("z2")
     w1b.start("x2")
     w1b.arrive("x")
+    for g in (w2a, w3b, w2b):
+        g.start("z")
     bias.arrive(2)
     bias.from_core(0, len(bias.core))
     l_h.wait()
@@ -595,17 +604,16 @@
         return step
 
     steps = {
-        (0, 0): [go(w3a, "y", "z2"), lambda: w3b.start("z"), go(w3b, "y", "z2")],
+        (0, 0): [go(w2b, "y", "z2"), lambda: w3a.start("z")],
         (0, 2): [go(w2a, "z", "x"), lambda: w1a.from_core("z", "x"), lambda: w1b.from_core("z", "x"), lambda: load(1, 1).start()],
         (0, 3): [go(w1b, "x2")],
-        (1, 1): [go(w2b, "z", "x")],
+        (1, 1): [go(w3b, "z", "y")],
         (1, 2): [go(w2a, "x", "y")],
-        (1, 3): [go(w1a, "y"), lambda: load(2, 0).start()],
-        (2, 1): [go(w3a, "z", "x"), go(w2b, "x", "y")],
-        (2, 2): [lambda: w1a.from_core("y"), lambda: w1b.from_core("z2", "x2"), lambda: load(3, 1).start()],
-        (3, 0): [go(w3a, "z2", "x2")],
-        (3, 1): [go(w3a, "x"), go(w2a, "y")],
-        (3, 3): [go(w3b, "z", "x")],
+        (1, 3): [go(w1a, "y"), lambda: load(2, 0).start(), go(w2b, "z", "x")],
+        (2, 1): [go(w3b, "y", "x")],
+        (2, 2): [lambda: w1a.from_core("y"), lambda: w1b.from_core("z2", "x2"), lambda: load(3, 1).start(), go(w2b, "z2", "x2")],
+        (3, 0): [go(w2b, "x"), go(w3a, "z", "y")],
+        (3, 2): [go(w2a, "y")],
     }
     load(0, 0).start()
 
@@ -653,9 +661,6 @@
         return 0
 
     lax.fori_loop(0, 4, group, 0)
-    w3a.arrive("x2")
-    w3b.arrive("z2")
-    w3b.start("x2")
     tiles = [jnp.zeros((16, 128), f32) for _ in range(6)]
     lane = lax.broadcasted_iota(jnp.int32, (1, 128), 1)
     for i in range(32):
@@ -667,13 +672,13 @@
             tiles[j + 1] = tiles[j + 1] + jnp.where(lane < r, piece, 0.0)
     for j in range(6):
         vec_ref[:, 128 * j : 128 * j + 128] = tiles[j]
-    w2b.arrive("y")
     w3b.arrive("x")
-    w3b.arrive("x2")
-    for g in (w2a, w2b):
-        g.from_core("z", "x", "y")
-    for g in (w3a, w3b):
-        g.from_core("z", "x", "z2", "x2")
+    w2b.arrive("x2")
+    w3a.arrive("y")
+    w2a.from_core("z", "x", "y")
+    w2b.from_core("z", "x", "z2", "x2")
+    w3a.from_core("z", "y")
+    w3b.from_core("z", "y", "x")
     for q in hx:
         q.wait_send()
     l_x.wait()
@@ -731,9 +736,15 @@
     l_h = local(heads_ref, hv, ls.at[1])
     l_wo = [local(g_ref.at[0, y, c, :, :, :, pl.ds(512, 256)], wo.at[2 * y + c], ls.at[2 + 2 * y + c]) for y in range(2) for c in range(2)]
     l_w2 = local(g_ref.at[1], w2, ls.at[6])
-    l_w3 = local(g_ref.at[2], w3, ls.at[7])
+    ra, rb = pl.ds(0, 48), pl.ds(48, 48)
+    parts = lambda r: (r.at[:, :, :, pc.x, ra], r.at[:, :, :, :, rb])
+    l_w3 = [local(a, b, ls.at[n]) for n, a, b in zip((7, 9), parts(g_ref.at[2]), parts(w3))]
     l_c = local(c_ref.at[pc.t], cv.at[pc.t], ls.at[8])
-    barrier([(pc.dp, pc.t ^ j) for j in (1, 2, 3)])
+    barrier([(pc.dp, pc.t ^ j) for j in (1, 2, 3)] + [pc.peer("x")])
+    came = w3.at[:, pc.c, :, 1 - pc.x, ra]
+    wx = rcopy(g_ref.at[2, :, pc.c, :, pc.x, ra], w3.at[:, pc.c, :, pc.x, ra], sems, pc.peer("x"))
+    wc = rcopy(came, came, sems, pc.peer("c"))
+    wx.start()
     cx = exchange(pc, c_ref, cv, sems)
     row = lambda n: vec_ref[n : n + 1, :]
     v_ref[...] = jnp.zeros_like(v_ref)
@@ -761,20 +772,38 @@
 
     lax.fori_loop(0, 4, first, 0)
     l_w2.wait()
-    l_w3.wait()
 
     def up(n, _):
         t, b = n // 4, n % 4
         rows = pl.ds(pl.multiple_of(b * 256, 256), 256)
         pre = dotf(low[rows, :], w2[t // 2, t % 2].reshape(768, 768)) + vec_ref[pl.ds(3 + t, 1), :]
         a, d = gelu_pair(pre)
-        a = a.astype(bf16)
-        act[t, rows, :] = a
+        act[t, rows, :] = a.astype(bf16)
         gd[t, rows, :] = d.astype(bf16)
-        acc[rows, :] += dot_nt(a, w3[t // 2, t % 2].reshape(768, 768))
+
+        @pl.when(n == 13)
+        def _():
+            wx.wait_recv()
+            wc.start()
+
         return 0
 
     lax.fori_loop(0, 16, up, 0)
+    wc.wait_recv()
+    for q in l_w3:
+        q.wait()
+
+    def branch(b, _):
+        rows = pl.ds(pl.multiple_of(b * 256, 256), 256)
+        total = acc[rows, :]
+        for t in range(4):
+            total = total + dot_nt(act[t, rows, :], w3[t // 2, t % 2].reshape(768, 768))
+        acc[rows, :] = total
+        return 0
+
+    lax.fori_loop(0, 4, branch, 0)
+    for q in (wx, wc):
+        q.wait_send()
     l_c.wait()
     for q in cx:
         q.wait()
@@ -866,7 +895,7 @@
             v_((4, 256, 768), bf16), v_((4, 256, 768), bf16), v_((4, L, 256), bf16), v_((4, 4, 2, 96, 256), bf16), wt, wt,
             v_((L, 768), f32), v_((L, 128), f32), v_((L, 768), bf16), v_((4, L, 768), bf16), v_((4, L, 768), bf16), v_((L, 768), f32),
             v_((L, 768), bf16), v_((768, L), bf16), v_((768, L), bf16), v_((4, 256, 768), bf16), v_((2, 2, 768, 768), bf16),
-            dma((9,)), dma((2, 2)), dma((6,)), dma((6,)),
+            dma((10,)), dma((2, 2)), dma((8,)), dma((8,)),
         ],
         compiler_params=pltpu.CompilerParams(collective_id=2, has_side_effects=True, vmem_limit_bytes=67043328),
     )(xs, cs, heads, g, vec)
@@ -923,9 +952,9 @@
     h, c = seqs(hidden_in), seqs(cotangent)
     my_prefix = lax.dynamic_slice_in_dim(prefix, t_me, 1, 0)
     if lax.axis_size("dp") == 8:
-        g, xs, vec, proj, projT, heads, ot, lse = front(my_prefix, s, h, vecs)
+        g, xs, vec, proj, projT, heads, ot, lse = front(prefix, s, h, vecs)
         oo, g1, g1low, doutw, d, v = mid(xs, c, heads, g, vec)
-        gs, vs, xx = back(my_prefix, xs, g1low, g1, g, proj, projT, ot, lse, doutw, d.reshape(2, 2, 2, 4, 2, rows, 768), v)
+        gs, vs, xx = back(prefix, xs, g1low, g1, g, proj, projT, ot, lse, doutw, d.reshape(2, 2, 2, 4, 2, rows, 768), v)
         qv = vs[16:24, :256].reshape(4, 2, 256)
         vs = jnp.concatenate([qv[:, 0, :192].reshape(1, 768), qv[:, 1, :192].reshape(1, 768), vs[2:16]])
     else:

time: 259 us -> 251 us (0.969)
  Pallas kernels: 238 us -> 231 us
    pallas_call x1, Pallas kernels: 94.9 us -> 86.9 us  [front(): pl.pallas_call(front_kernel, out_shape=[sd((3, 2, 2, 4, 2, 96, 768), bf16...]
    unnamed x20 -> x26, local copies, waits for them, and re-layouts: 13.2 us -> 13.7 us
where the time goes in v3:
time: 251 us
  Pallas kernels  231 us (92%)
  local copies, waits for them, and re-layouts  17.3 us (7%)
    pallas_call x1, Pallas kernels, front(): pl.pallas_call(front_kernel, out_shape=[sd((3, 2, 2, 4, 2, 96, 768), bf16...  86.9 us
    pallas_call x1, Pallas kernels, back(): pl.pallas_call(back_kernel, out_shape=[sd((3, 96, 768), f32), sd((24, 768...  86.8 us
    pallas_call x1, Pallas kernels, mid(): pl.pallas_call(mid_kernel, out_shape=[sd((4, 256, 768), bf16), sd((L, 768...  57.5 us
    unnamed x26, local copies, waits for them, and re-layouts  13.7 us

profile of v3, /device:TPU:0, one launch (start us, length us, event | category | flops | bytes accessed | tf_op | source)
XLA Modules:
  0.0 250.9 jit_solution(1094944097502881484)
XLA Ops:
  0.6 0.0 copy-start.4
  0.6 0.0 copy-start.5
  0.7 0.0 copy-start.3
  0.7 0.0 copy-start.2
  0.7 2.8 %copy.44 = bf16[256,4,768]{2,0,1:T(8,128)(2,1)} copy(bf16[256,4,768]{2,1,0:T(4,128)(2,1)} %param.9) | data formatting | bytes 3145728 | tf_op args[0]
  3.5 0.0 copy-start.7
  3.5 0.0 copy-start.8
  3.5 0.0 copy-done.4
  3.5 0.2 copy.27
  3.6 0.2 copy.29
  3.8 0.0 copy-done.5
  3.8 0.1 copy.28
  3.9 0.1 maximum_bitcast_fusion
  4.0 0.0 copy-done.3
  4.0 0.0 copy-done.2
  4.0 0.8 pad_maximum_fusion.s_ref
  4.8 0.0 copy-done.7
  4.8 0.0 copy-done.8
  4.8 0.6 select_maximum_fusion.b_ref
  5.5 86.9 %shard_map.152 = (bf16[3,2,2,4,2,96,768]{6,5,4,3,2,1,0:T(8,128)(2,1)}, bf16[4,256,768]{2,1,0:T(8,128)(2,1)}, f32[16,768]{1,0:T(8,128)}, bf16[4,1024,640]{2,1,0:T...) custom-call(s32[4]{0:T(128)} %prefix_ref.3, ...), custom_call_target="tpu_custom_call" | custom-call | tf_op jit(solution)/shard_map/pallas_call | solution.py:697
  92.4 2.7 %copy.43 = bf16[256,4,768]{2,0,1:T(8,128)(2,1)} copy(bf16[256,4,768]{2,1,0:T(4,128)(2,1)} %param.10) | data formatting | bytes 3145728 | tf_op args[1]
  95.2 57.5 %shard_map.153 = (bf16[4,256,768]{2,1,0:T(8,128)(2,1)}, f32[1024,768]{1,0:T(8,128)}, bf16[1024,768]{1,0:T(8,128)(2,1)}, bf16[4,768,256]{2,1,0:T(8,128)(2,1)}, bf...) custom-call(bf16[4,256,768]{2,1,0:T(8,128)(2,1)} %get-tuple-element.25.x_ref, bf16[4,256,768]{2,1,0:T(8,128)(2,1)} %bitcast.31, ...), custom_call_target="tpu_custom_call" | custom-call | tf_op jit(solution)/shard_map/pallas_call | solution.py:889
  152.6 86.8 %shard_map.154 = (f32[3,96,768]{2,1,0:T(8,128)}, f32[24,768]{1,0:T(8,128)}, bf16[4,256,768]{2,1,0:T(8,128)(2,1)}) custom-call(s32[4]{0:T(128)} %prefix_ref.3, bf16[4,256,768]{2,1,0:T(8,128)(2,1)} %get-tuple-element.25.x_ref, bf16[1024,768]{1,0:T(8,128)(2,1)} %get-tuple-element.30.g_ref, f32[1024,768]{1,0:T(8,128)} %get-tuple-element.31.gf_ref, ...), custom_call_target="tpu_custom_call" | custom-call | tf_op jit(solution)/shard_map/pallas_call | solution.py:410
  239.5 0.9 slice.37
  240.4 0.7 slice.34
  241.1 0.1 reshape_squeeze.10
  241.2 0.1 reshape_squeeze.11
  241.3 0.1 fusion.1
  241.4 0.0 copy-start.6
  241.4 0.6 slice.43
  241.9 0.0 copy-start.1
  241.9 3.8 %copy.36 = bf16[256,4,768]{2,1,0:T(4,128)(2,1)} copy(bf16[256,4,768]{2,0,1:T(8,128)(2,1)} %bitcast.33) | data formatting | bytes 3145728
  245.8 0.0 copy-done.6
  245.8 0.0 copy-done.1
  245.8 0.0 copy-start
  245.8 0.1 copy.32
  245.9 0.9 copy.37
  246.8 0.8 slice_bitcast_fusion
  247.7 0.1 slice_bitcast_fusion.2
  247.8 0.7 copy.38
  248.5 0.0 copy-done
  248.5 2.4 copy.35
  (3 shorter events, 0.1 us)
Async XLA Ops:
  0.6 2.8 %copy-start.4 = (bf16[96,3,192]{2,0,1:T(8,128)(2,1)S(1)}, bf16[96,3,192]{2,0,1:T(8,128)(2,1)}, u32[]{:S(2)}) copy-start(bf16[96,3,192]{2,0,1:T(8,128)(2,1)} %param.12) | copy-start | bytes 331780
  0.6 3.2 %copy-start.5 = (bf16[192,96]{1,0:T(8,128)(2,1)S(1)}, bf16[192,96]{1,0:T(8,128)(2,1)}, u32[]{:S(2)}) copy-start(bf16[192,96]{1,0:T(8,128)(2,1)} %param.13) | copy-start | bytes 110596
  0.7 3.4 %copy-start.3 = (bf16[96,768]{1,0:T(8,128)(2,1)S(1)}, bf16[96,768]{1,0:T(8,128)(2,1)}, u32[]{:S(2)}) copy-start(bf16[96,768]{1,0:T(8,128)(2,1)} %param.14) | copy-start | bytes 442372
  0.7 3.4 %copy-start.2 = (bf16[768,96]{0,1:T(8,128)(2,1)S(1)}, bf16[768,96]{0,1:T(8,128)(2,1)}, u32[]{:S(2)}) copy-start(bf16[768,96]{0,1:T(8,128)(2,1)} %param.15) | copy-start | bytes 442372
  3.5 1.4 copy-start.7
  3.5 1.4 copy-start.8
  241.4 4.4 %copy-start.6 = (f32[16,24]{1,0:T(8,128)}, f32[16,24]{1,0:T(8,128)S(1)}, u32[]{:S(2)}) copy-start(f32[16,24]{1,0:T(8,128)S(1)} %fusion.1) | copy-start | bytes 4612
  241.9 3.9 %copy-start.1 = (f32[3,96,768]{2,1,0:T(8,128)S(1)}, f32[3,96,768]{2,1,0:T(8,128)}, u32[]{:S(2)}) copy-start(f32[3,96,768]{2,1,0:T(8,128)} %get-tuple-element.40) | copy-start | bytes 2654212
  245.8 2.7 %copy-start = (bf16[4,256,768]{2,1,0:T(8,128)(2,1)S(1)}, bf16[4,256,768]{2,1,0:T(8,128)(2,1)}, u32[]{:S(2)}) copy-start(bf16[4,256,768]{2,1,0:T(8,128)(2,1)} %get-tuple-element.29) | copy-start | bytes 4718596

commit v4 on v3

--- a/solution.py
+++ b/solution.py
@@ -580,11 +580,12 @@
     w1b.start("x")
     w1a.arrive("x")
     w1a.start("y")
+    w2a.start("z")
+    w3b.start("z")
     w1b.arrive("z2")
     w1b.start("x2")
     w1b.arrive("x")
-    for g in (w2a, w3b, w2b):
-        g.start("z")
+    w2b.start("z")
     bias.arrive(2)
     bias.from_core(0, len(bias.core))
     l_h.wait()

time: 251 us -> 250 us (level)
  no operation moved by 1% of the time
where the time goes in v4:
time: 250 us; the launch traced here: 249 us
  Pallas kernels  230 us (92%)
  local copies, waits for them, and re-layouts  17.3 us (7%)
    pallas_call x1, Pallas kernels, back(): pl.pallas_call(back_kernel, out_shape=[sd((3, 96, 768), f32), sd((24, 768...  86.9 us
    pallas_call x1, Pallas kernels, front(): pl.pallas_call(front_kernel, out_shape=[sd((3, 2, 2, 4, 2, 96, 768), bf16...  85.6 us
    pallas_call x1, Pallas kernels, mid(): pl.pallas_call(mid_kernel, out_shape=[sd((4, 256, 768), bf16), sd((L, 768...  57 us
    unnamed x26, local copies, waits for them, and re-layouts  13.7 us

profile of v4, /device:TPU:0, one launch (start us, length us, event | category | flops | bytes accessed | tf_op | source)
XLA Modules:
  0.0 249.2 jit_solution(11034269842211070665)
XLA Ops:
  0.6 0.0 copy-start.4
  0.6 0.0 copy-start.5
  0.7 0.0 copy-start.3
  0.7 0.0 copy-start.2
  0.7 2.8 %copy.44 = bf16[256,4,768]{2,0,1:T(8,128)(2,1)} copy(bf16[256,4,768]{2,1,0:T(4,128)(2,1)} %param.9) | data formatting | bytes 3145728 | tf_op args[0]
  3.5 0.0 copy-start.7
  3.5 0.0 copy-start.8
  3.5 0.0 copy-done.4
  3.5 0.2 copy.27
  3.6 0.2 copy.29
  3.8 0.0 copy-done.5
  3.8 0.1 copy.28
  3.9 0.1 maximum_bitcast_fusion
  4.0 0.0 copy-done.3
  4.0 0.0 copy-done.2
  4.0 0.8 pad_maximum_fusion.s_ref
  4.8 0.0 copy-done.7
  4.8 0.0 copy-done.8
  4.8 0.6 select_maximum_fusion.b_ref
  5.5 85.6 %shard_map.152 = (bf16[3,2,2,4,2,96,768]{6,5,4,3,2,1,0:T(8,128)(2,1)}, bf16[4,256,768]{2,1,0:T(8,128)(2,1)}, f32[16,768]{1,0:T(8,128)}, bf16[4,1024,640]{2,1,0:T...) custom-call(s32[4]{0:T(128)} %prefix_ref.3, ...), custom_call_target="tpu_custom_call" | custom-call | tf_op jit(solution)/shard_map/pallas_call | solution.py:698
  91.1 2.7 %copy.43 = bf16[256,4,768]{2,0,1:T(8,128)(2,1)} copy(bf16[256,4,768]{2,1,0:T(4,128)(2,1)} %param.10) | data formatting | bytes 3145728 | tf_op args[1]
  93.8 57.0 %shard_map.153 = (bf16[4,256,768]{2,1,0:T(8,128)(2,1)}, f32[1024,768]{1,0:T(8,128)}, bf16[1024,768]{1,0:T(8,128)(2,1)}, bf16[4,768,256]{2,1,0:T(8,128)(2,1)}, bf...) custom-call(bf16[4,256,768]{2,1,0:T(8,128)(2,1)} %get-tuple-element.25.x_ref, bf16[4,256,768]{2,1,0:T(8,128)(2,1)} %bitcast.31, ...), custom_call_target="tpu_custom_call" | custom-call | tf_op jit(solution)/shard_map/pallas_call | solution.py:890
  150.8 86.9 %shard_map.154 = (f32[3,96,768]{2,1,0:T(8,128)}, f32[24,768]{1,0:T(8,128)}, bf16[4,256,768]{2,1,0:T(8,128)(2,1)}) custom-call(s32[4]{0:T(128)} %prefix_ref.3, bf16[4,256,768]{2,1,0:T(8,128)(2,1)} %get-tuple-element.25.x_ref, bf16[1024,768]{1,0:T(8,128)(2,1)} %get-tuple-element.30.g_ref, f32[1024,768]{1,0:T(8,128)} %get-tuple-element.31.gf_ref, ...), custom_call_target="tpu_custom_call" | custom-call | tf_op jit(solution)/shard_map/pallas_call | solution.py:410
  237.8 0.9 slice.37
  238.7 0.7 slice.34
  239.4 0.1 reshape_squeeze.10
  239.5 0.1 reshape_squeeze.11
  239.6 0.1 fusion.1
  239.7 0.0 copy-start.6
  239.7 0.6 slice.43
  240.2 0.0 copy-start.1
  240.2 3.8 %copy.36 = bf16[256,4,768]{2,1,0:T(4,128)(2,1)} copy(bf16[256,4,768]{2,0,1:T(8,128)(2,1)} %bitcast.33) | data formatting | bytes 3145728
  244.1 0.0 copy-done.6
  244.1 0.0 copy-done.1
  244.1 0.0 copy-start
  244.1 0.1 copy.32
  244.2 0.9 copy.37
  245.1 0.8 slice_bitcast_fusion
  246.0 0.1 slice_bitcast_fusion.2
  246.1 0.7 copy.38
  246.8 0.0 copy-done
  246.8 2.4 copy.35
  (3 shorter events, 0.1 us)
Async XLA Ops:
  0.6 2.8 %copy-start.4 = (bf16[96,3,192]{2,0,1:T(8,128)(2,1)S(1)}, bf16[96,3,192]{2,0,1:T(8,128)(2,1)}, u32[]{:S(2)}) copy-start(bf16[96,3,192]{2,0,1:T(8,128)(2,1)} %param.12) | copy-start | bytes 331780
  0.6 3.2 %copy-start.5 = (bf16[192,96]{1,0:T(8,128)(2,1)S(1)}, bf16[192,96]{1,0:T(8,128)(2,1)}, u32[]{:S(2)}) copy-start(bf16[192,96]{1,0:T(8,128)(2,1)} %param.13) | copy-start | bytes 110596
  0.7 3.4 %copy-start.3 = (bf16[96,768]{1,0:T(8,128)(2,1)S(1)}, bf16[96,768]{1,0:T(8,128)(2,1)}, u32[]{:S(2)}) copy-start(bf16[96,768]{1,0:T(8,128)(2,1)} %param.14) | copy-start | bytes 442372
  0.7 3.4 %copy-start.2 = (bf16[768,96]{0,1:T(8,128)(2,1)S(1)}, bf16[768,96]{0,1:T(8,128)(2,1)}, u32[]{:S(2)}) copy-start(bf16[768,96]{0,1:T(8,128)(2,1)} %param.15) | copy-start | bytes 442372
  3.5 1.4 copy-start.7
  3.5 1.4 copy-start.8
  239.7 4.4 %copy-start.6 = (f32[16,24]{1,0:T(8,128)}, f32[16,24]{1,0:T(8,128)S(1)}, u32[]{:S(2)}) copy-start(f32[16,24]{1,0:T(8,128)S(1)} %fusion.1) | copy-start | bytes 4612
  240.2 3.9 %copy-start.1 = (f32[3,96,768]{2,1,0:T(8,128)S(1)}, f32[3,96,768]{2,1,0:T(8,128)}, u32[]{:S(2)}) copy-start(f32[3,96,768]{2,1,0:T(8,128)} %get-tuple-element.40) | copy-start | bytes 2654212
  244.1 2.7 %copy-start = (bf16[4,256,768]{2,1,0:T(8,128)(2,1)S(1)}, bf16[4,256,768]{2,1,0:T(8,128)(2,1)}, u32[]{:S(2)}) copy-start(bf16[4,256,768]{2,1,0:T(8,128)(2,1)} %get-tuple-element.29) | copy-start | bytes 4718596
